TPU v7x, 512 devices: a whole 4x8x8 slice. The times are simulated.
512 devices in a mesh: req: 128 (over z, y, core), tp: 4 (over x).
Axes of the slice: x: 4, y: 8, z: 8, core: 2. Of those that a mesh axis runs over, the one named last changes fastest.
Arguments:
- hidden_in: bfloat16 [128, 128, 1024], P('req', 'tp'), may hold values from -6 to 6
- cache_keys: bfloat16 [128, 4096, 512], P('req', None, 'tp'), may hold values from -6 to 6
- cache_values: bfloat16 [128, 4096, 512], P('req', None, 'tp'), may hold values from -6 to 6
- lengths: int32 [128], replicated, may hold values from 0 to 4096, as said below
- request_order: int32 [128], replicated, may hold values from 0 to 127, each once
- routes: int32 [128, 128, 8], P('req'), may hold values from 0 to 31, all different within a row; in each aligned block of 32 rows (0 to 31, 32 to 63, ..., all dimensions but the last counted through in order) at most 12 rows name the same one
- query_weight: bfloat16 [1024, 1024], P(None, 'tp'), may hold values from -0.1875 to 0.1875
- key_weight: bfloat16 [1024, 512], P(None, 'tp'), may hold values from -0.1875 to 0.1875
- value_weight: bfloat16 [1024, 512], P(None, 'tp'), may hold values from -0.1875 to 0.1875
- out_weight: bfloat16 [1024, 1024], P('tp'), may hold values from -0.1875 to 0.1875
- attention_gain: float32 [1024], replicated, may hold values from 0.1 to 1.9
- expert_gain: float32 [1024], replicated, may hold values from 0.1 to 1.9
- router_weight: bfloat16 [1024, 32], replicated, may hold values from -0.1875 to 0.1875
- gate_weight: bfloat16 [128, 1024, 512], P('req', None, 'tp'), may hold values from -0.125 to 0.125, as said below
- up_weight: bfloat16 [128, 1024, 512], P('req', None, 'tp'), may hold values from -0.125 to 0.125, as said below
- down_weight: bfloat16 [128, 512, 1024], P('req', 'tp'), may hold values from -0.176776695 to 0.176776695, as said below
- final_gain: float32 [1024], replicated, may hold values from 0.1 to 1.9
- vocab_weight: bfloat16 [1024, 49152], P(None, ('req', 'tp')), may hold values from -0.1875 to 0.1875
Outputs:
- layer_out: bfloat16 [128, 128, 1024], P('req', 'tp')
- logits: float32 [128, 49152], P(None, ('req', 'tp'))
Inputs may be any that keep to these rules, and one draw needn't show every extreme that they name: Slot r's cache holds valid keys and values at positions below lengths[r]; some slot's length is 4096. `request_order`: each request is held by exactly one slot. `routes`: each token names 8 different experts; in each aligned block of 32 tokens of a slot no expert is named by more than 12 tokens, and some expert reaches 12. `gate_weight`: stored copies k * 4 to k * 4 + 3 are equal and hold expert k. `up_weight`: stored copies k * 4 to k * 4 + 3 are equal and hold expert k. `down_weight`: stored copies k * 4 to k * 4 + 3 are equal and hold expert k.
All inputs are finite; a program needn't handle non-finite values.
Results may differ from a plain program's by a relative error of at most 0.015.
Values may be sent and summed in bfloat16 or wider, within the bound.
A program may use at most 64 MiB of HBM per device.

v0:
```python
import jax
import jax.numpy as jnp
from jax import lax
from jax.sharding import PartitionSpec as P

HEAD_DIM = 64
EXPERTS = 32
TOPK = 8
SPAN = 128


epsilon = 1e-06
key_block = 512


def rms_scale(row_block, gain_vector):
    widened = row_block.astype(jnp.float32)
    return (
        widened
        * lax.rsqrt(jnp.mean(widened * widened, axis=-1, keepdims=True) + epsilon)
        * gain_vector
    )


def rotate(values, positions):
    half_dim = values.shape[-1] // 2
    frequency = jnp.exp(
        -jnp.log(10000.0) * jnp.arange(half_dim, dtype=jnp.float32) * (2.0 / values.shape[-1])
    )
    angles = positions.astype(jnp.float32)[:, None] * frequency[None, :]
    cosine_table = jnp.cos(angles)[:, None, :]
    sine_table = jnp.sin(angles)[:, None, :]
    front_half = values[..., :half_dim]
    back_half = values[..., half_dim:]
    return jnp.concatenate(
        [
            front_half * cosine_table - back_half * sine_table,
            back_half * cosine_table + front_half * sine_table,
        ],
        axis=-1,
    )


def cache_attend(queries, key_rows, value_rows, lowest, highest):
    token_count, key_heads, group_size, head_size = queries.shape
    window = min(key_block, key_rows.shape[0])
    score_scale = head_size ** (-0.5)

    def block_step(block_number, running):
        numerator, denominator = running
        offset = block_number * window
        block_keys = lax.dynamic_slice_in_dim(key_rows, offset, window, 0).reshape(
            window, key_heads, head_size
        )
        block_values = lax.dynamic_slice_in_dim(value_rows, offset, window, 0).reshape(
            window, key_heads, head_size
        )
        scores = (
            jnp.einsum("ckgd,jkd->ckgj", queries, block_keys, preferred_element_type=jnp.float32)
            * score_scale
        )
        key_places = offset + jnp.arange(window, dtype=jnp.int32)
        inside = (key_places >= lowest) & (key_places < highest)
        exp_scores = jnp.where(inside, jnp.exp(scores), 0.0)
        numerator = numerator + jnp.einsum(
            "ckgj,jkd->ckgd",
            exp_scores.astype(jnp.bfloat16),
            block_values,
            preferred_element_type=jnp.float32,
        )
        return (numerator, denominator + jnp.sum(exp_scores, axis=-1))

    first_block = lowest // window
    last_block = (highest + window - 1) // window
    initial = (
        jnp.zeros((token_count, key_heads, group_size, head_size), jnp.float32),
        jnp.zeros((token_count, key_heads, group_size), jnp.float32),
    )
    return lax.fori_loop(first_block, last_block, block_step, initial)


def body(
    hidden_in,
    cache_keys,
    cache_values,
    lengths,
    request_order,
    routes,
    query_weight,
    key_weight,
    value_weight,
    out_weight,
    attention_gain,
    expert_gain,
    router_weight,
    gate_weight,
    up_weight,
    down_weight,
    final_gain,
    vocab_weight,
):
    lane_count = lax.axis_size("tp")
    req_count = lax.axis_size("req")
    lane_index = lax.axis_index("tp")
    slot_index = lax.axis_index("req")
    own_rows = hidden_in[0]
    shard_rows = own_rows.shape[0]
    model_width = own_rows.shape[1]
    query_width = query_weight.shape[1]
    key_width = key_weight.shape[1]
    key_heads = key_width // HEAD_DIM
    group_size = query_width // key_width
    attn_in = rms_scale(own_rows, attention_gain).astype(jnp.bfloat16)
    joined = jnp.concatenate([query_weight, key_weight, value_weight], axis=1)
    projected = jnp.dot(
        lax.all_gather(attn_in, "tp", axis=0, tiled=True),
        joined,
        preferred_element_type=jnp.float32,
    )
    my_length = lengths[slot_index]
    positions = my_length + jnp.arange(SPAN, dtype=jnp.int32)
    queries = (
        rotate(
            projected[:, :query_width].reshape(SPAN, key_heads * group_size, HEAD_DIM), positions
        )
        .astype(jnp.bfloat16)
        .reshape(SPAN, key_heads, group_size, HEAD_DIM)
    )
    new_keys = rotate(
        projected[:, query_width : query_width + key_width].reshape(SPAN, key_heads, HEAD_DIM),
        positions,
    ).astype(jnp.bfloat16)
    new_values = (
        projected[:, query_width + key_width :]
        .astype(jnp.bfloat16)
        .reshape(SPAN, key_heads, HEAD_DIM)
    )
    score_scale = HEAD_DIM ** (-0.5)
    token_range = jnp.arange(SPAN, dtype=jnp.int32)
    causal = token_range[None, :] <= token_range[:, None]
    span_scores = (
        jnp.einsum("ckgd,jkd->ckgj", queries, new_keys, preferred_element_type=jnp.float32)
        * score_scale
    )
    span_expo = jnp.where(causal[:, None, None, :], jnp.exp(span_scores), 0.0)
    numerator = jnp.einsum(
        "ckgj,jkd->ckgd",
        span_expo.astype(jnp.bfloat16),
        new_values,
        preferred_element_type=jnp.float32,
    )
    denominator = jnp.sum(span_expo, axis=-1)
    own_keys = cache_keys[0]
    own_values = cache_values[0]
    own_numer, own_denom = cache_attend(queries, own_keys, own_values, 0, my_length)
    numerator = numerator + own_numer
    denominator = denominator + own_denom
    attended = (numerator / denominator[..., None]).astype(jnp.bfloat16).reshape(SPAN, query_width)
    attention_sum = lax.psum_scatter(
        jnp.dot(attended, out_weight, preferred_element_type=jnp.float32).astype(jnp.bfloat16),
        "tp",
        scatter_dimension=0,
        tiled=True,
    ).astype(jnp.float32)
    mixed_rows = (own_rows.astype(jnp.float32) + attention_sum).astype(jnp.bfloat16)
    expert_in = rms_scale(mixed_rows, expert_gain).astype(jnp.bfloat16)
    expert_rows = lax.all_gather(expert_in, "tp", axis=0, tiled=True)
    router_logits = jnp.dot(expert_rows, router_weight, preferred_element_type=jnp.float32)
    route_ids = routes[0]
    chosen = route_ids[:, :, None] == jnp.arange(EXPERTS, dtype=jnp.int32)
    picked = jnp.sum(jnp.where(chosen, router_logits[:, None, :], 0.0), axis=-1)
    gate_expo = jnp.exp(picked)
    gate_values = (gate_expo / jnp.sum(gate_expo, axis=-1, keepdims=True)).astype(jnp.bfloat16)
    replicas = max(1, req_count // EXPERTS)
    block_len = SPAN // replicas
    capacity = 3 * block_len * TOPK // (2 * EXPERTS)
    local_experts = gate_weight.shape[0]
    share_size = capacity // lane_count
    counts = jnp.sum(chosen.astype(jnp.int32), axis=1)
    blocked = counts.reshape(replicas, block_len, EXPERTS)
    rank_table = (jnp.cumsum(blocked, axis=1) - blocked).reshape(SPAN, EXPERTS)
    rank_pick = jnp.sum(jnp.where(chosen, rank_table[:, None, :], 0), axis=-1)
    block_id = token_range // block_len
    slot_ids = ((route_ids * replicas + block_id[:, None]) * capacity + rank_pick).reshape(-1)
    slot_total = req_count * local_experts * capacity
    token_ids = jnp.repeat(token_range, TOPK)
    slot_token = jnp.full((slot_total,), SPAN, jnp.int32).at[slot_ids].set(token_ids)
    slot_gate = jnp.zeros((slot_total,), jnp.bfloat16).at[slot_ids].set(gate_values.reshape(-1))
    outgoing = jnp.take(expert_rows, slot_token, axis=0, mode="fill", fill_value=0).reshape(
        req_count, local_experts, capacity, model_width
    )
    arrived = lax.all_to_all(outgoing, "req", split_axis=0, concat_axis=0, tiled=True)
    gate_part = jnp.einsum(
        "necd,edf->necf", arrived, gate_weight, preferred_element_type=jnp.float32
    )
    up_part = jnp.einsum("necd,edf->necf", arrived, up_weight, preferred_element_type=jnp.float32)
    unit_hidden = (jax.nn.silu(gate_part) * up_part).astype(jnp.bfloat16)
    partial_value = jnp.einsum(
        "necf,efd->necd", unit_hidden, down_weight, preferred_element_type=jnp.float32
    )
    unit_sum = lax.psum_scatter(
        partial_value.astype(jnp.bfloat16), "tp", scatter_dimension=2, tiled=True
    )
    returned = lax.all_to_all(unit_sum, "req", split_axis=0, concat_axis=0, tiled=True)
    lane_tokens = lax.dynamic_slice_in_dim(
        slot_token.reshape(req_count, local_experts, capacity),
        lane_index * share_size,
        share_size,
        2,
    ).reshape(-1)
    lane_gates = lax.dynamic_slice_in_dim(
        slot_gate.reshape(req_count, local_experts, capacity),
        lane_index * share_size,
        share_size,
        2,
    ).reshape(-1)
    combine = jnp.where(
        lane_tokens[None, :] == token_range[:, None],
        lane_gates[None, :],
        jnp.zeros((), jnp.bfloat16),
    )
    flat_back = returned.reshape(-1, model_width)
    expert_sum = lax.psum_scatter(
        jnp.dot(combine, flat_back, preferred_element_type=jnp.float32).astype(jnp.bfloat16),
        "tp",
        scatter_dimension=0,
        tiled=True,
    ).astype(jnp.float32)
    layer_rows = (mixed_rows.astype(jnp.float32) + expert_sum).astype(jnp.bfloat16)
    tail_row = layer_rows[shard_rows - 1 :]
    every_tail = lax.all_gather(tail_row, ("req", "tp"), axis=0, tiled=True).reshape(
        req_count, lane_count, model_width
    )[:, lane_count - 1]
    final_in = rms_scale(every_tail, final_gain).astype(jnp.bfloat16)
    slot_logits = jnp.dot(final_in, vocab_weight, preferred_element_type=jnp.float32)
    inverse = (
        jnp.zeros((req_count,), jnp.int32)
        .at[request_order]
        .set(jnp.arange(req_count, dtype=jnp.int32))
    )
    logits = jnp.take(slot_logits, inverse, axis=0)
    return (layer_rows[None], logits)


def solution(mesh):
    in_specs = (
        P("req", "tp", None),
        P("req", None, "tp"),
        P("req", None, "tp"),
        P(),
        P(),
        P("req", None, None),
        P(None, "tp"),
        P(None, "tp"),
        P(None, "tp"),
        P("tp", None),
        P(),
        P(),
        P(),
        P("req", None, "tp"),
        P("req", None, "tp"),
        P("req", "tp", None),
        P(),
        P(None, ("req", "tp")),
    )
    out_specs = (P("req", "tp", None), P(None, ("req", "tp")))
    return jax.shard_map(body, mesh=mesh, in_specs=in_specs, out_specs=out_specs, check_vma=False)
```

profile of v0, /device:TPU:1, one launch (start us, length us, event | category | flops | bytes accessed | tf_op | source)
XLA Modules:
  0.0 472.9 jit_solution(13799413404447211375)
XLA Ops:
  7.2 1.3 dynamic_slice.15
  9.9 1.0 fusion.65
  10.9 0.9 fusion.67
  11.8 10.5 %all_gather.9 = bf16[128,1024]{1,0:T(8,128)(2,1)S(1)} all-gather(bf16[32,1024]{1,0:T(8,128)(2,1)S(1)} %fusion.67), channel_id=1, replica_groups=mesh['req'=128,'tp'=4] {'tp'}, dimensions={0}, use_global_device_ids=true | all-gather | bytes 327680 | tf_op jit(solution)/shard_map/all_gather | solution.py:116
  22.4 1.5 fusion.35
  25.0 1.5 copy.70
  26.6 1.4 while.12
  28.5 0.9 convolution_convert_fusion
  29.6 1.0 scatter_custom_fusion.2
  31.6 4.3 scatter_custom_fusion
  36.1 28.6 %reduce-scatter.4.cloned.1.call-done = bf16[32,1024]{1,0:T(8,128)(2,1)} async-done(((bf16[128,1024]{1,0:T(8,128)(2,1)}), bf16[32,1024]{1,0:T(8,128)(2,1)}) %reduce-scatter.4.cloned.1.call-update) | async-done | bytes 65552 | tf_op jit(solution)/shard_map/reduce_scatter | solution.py:159
  64.7 1.0 fusion.61
  65.7 0.9 fusion.63
  66.6 9.4 %all_gather.10 = bf16[128,1024]{1,0:T(8,128)(2,1)S(1)} all-gather(bf16[32,1024]{1,0:T(8,128)(2,1)S(1)} %fusion.63), channel_id=1, replica_groups=mesh['req'=128,'tp'=4] {'tp'}, dimensions={0}, use_global_device_ids=true | all-gather | bytes 327680 | tf_op jit(solution)/shard_map/all_gather | solution.py:167
  76.0 5.8 %gather_fusion = bf16[1536,1024]{1,0:T(8,128)(2,1)} fusion(bf16[128,1024]{1,0:T(8,128)(2,1)S(1)} %all_gather.10, s32[2048]{0:T(1024)S(1)} %pad_clamp_fusion), kind=kCustom, calls=%fused_computation | custom fusion | bytes 6297600 | tf_op jit(solution)/shard_map/jit(_take)/gather | solution.py:189
  81.8 6.1 %gather.11 = bf16[128,1,12,1024]{3,2,0,1:T(8,128)(2,1)} reshape(bf16[1536,1024]{1,0:T(8,128)(2,1)} %gather_fusion) | data formatting | bytes 6291456 | tf_op jit(solution)/shard_map/jit(_take)/gather | solution.py:189
  87.9 2.5 select_bitcast_fusion
  90.4 115.1 %all_to_all.10 = bf16[128,1,12,1024]{3,2,1,0:T(8,128)(2,1)S(1)} all-to-all(bf16[128,1,12,1024]{3,2,1,0:T(8,128)(2,1)S(1)} %select_bitcast_fusion), channel_id=1, replica_groups=mesh['req'=128,'tp'=4] {'req'}, dimensions={0} | all-to-all | bytes 6291456 | tf_op jit(solution)/shard_map/all_to_all | solution.py:192
  205.5 1.9 copy-done.1
  207.5 3.5 fusion.14
  211.0 8.9 %convert_bitcast_fusion = bf16[128,1,12,1024]{3,0,2,1:T(8,128)(2,1)} fusion(bf16[128,1,12,1024]{3,2,1,0:T(8,128)(2,1)} %copy-done.1, f32[128,1,12,128]{3,0,2,1:T(8,128)S(1)} %fusion.14, bf16[1,128,1024]{2,1,0:T(8,128)(2,1)S(1)} %copy-done.12, bf16[1,1024,128]{2,1,0:T(8,128)(2,1)S(1)} %copy-done.13), kind=kOutput, calls=%fused_computation.23 | convolution fusion | flops 808058880 | bytes 7602176 | tf_op jit(solution)/shard_map/necf,efd->necd/dot_general | solution.py:198
  219.9 47.2 %reduce-scatter.6.cloned.1.call-done = bf16[128,1,3,1024]{3,0,2,1:T(8,128)(2,1)} async-done(((bf16[128,1,12,1024]{3,0,2,1:T(8,128)(2,1)}), bf16[128,1,3,1024]{3,0,2,1:T(8,128)(2,1)}) %reduce-scatter.6.cloned.1.call-update) | async-done | bytes 786448 | tf_op jit(solution)/shard_map/reduce_scatter | solution.py:201
  267.1 2.8 copy.79
  269.9 14.5 %all-to-all-start.1 = ((bf16[128,1,3,1024]{3,2,1,0:T(4,128)(2,1)}), bf16[128,1,3,1024]{3,2,1,0:T(4,128)(2,1)S(1)}, u32[]{:S(2)}, u32[]{:S(2)}) async-start(bf16[128,1,3,1024]{3,2,1,0:T(4,128)(2,1)} %copy.79), calls=%async_computation.3 | async-start | bytes 2097152 | tf_op jit(solution)/shard_map/all_to_all | solution.py:204
  285.6 7.6 %scatter_custom_fusion.1 = bf16[1536]{0:T(1024)(128)(2,1)S(1)} fusion(s32[1024]{0:T(1024)S(1)} %bitcast.191, bf16[1024]{0:T(1024)(128)(2,1)S(1)} %reshape.317, bf16[]{:T(256)} %constant.122.clone.1), kind=kCustom, calls=%fused_computation.114 | custom fusion | bytes 3074 | tf_op jit(solution)/shard_map/scatter | solution.py:188
  293.6 21.8 %all-to-all-done.1 = bf16[128,1,3,1024]{3,2,1,0:T(4,128)(2,1)S(1)} async-done(((bf16[128,1,3,1024]{3,2,1,0:T(4,128)(2,1)}), bf16[128,1,3,1024]{3,2,1,0:T(4,128)(2,1)S(1)}, u32[]{:S(2)}, u32[]{:S(2)}) %all-to-all-start.1) | async-done | bytes 786464 | tf_op jit(solution)/shard_map/all_to_all | solution.py:204
  316.0 1.0 convolution_convert_fusion.1
  317.1 15.9 %reduce-scatter.8.cloned.1.call-done = bf16[32,1024]{1,0:T(8,128)(2,1)} async-done(((bf16[128,1024]{1,0:T(8,128)(2,1)}), bf16[32,1024]{1,0:T(8,128)(2,1)}) %reduce-scatter.8.cloned.1.call-update) | async-done | bytes 65552 | tf_op jit(solution)/shard_map/reduce_scatter | solution.py:223
  333.0 0.9 fusion.64
  334.5 121.5 %all-gather.3.cloned.1.call-done = bf16[512,1,1024]{2,1,0:T(2,128)(2,1)} async-done(((bf16[1,1,1024]{2,1,0:T(2,128)(2,1)}), bf16[512,1,1024]{2,1,0:T(2,128)(2,1)}) %all-gather.3.cloned.1.call-update) | async-done | bytes 1048592 | tf_op jit(solution)/shard_map/all_gather | solution.py:231
  456.0 7.4 %reduce = bf16[512,1024]{1,0:T(8,128)(2,1)S(1)} reduce(bf16[512,1,1024]{2,1,0:T(2,128)(2,1)} %all-gather.3.cloned.1.call-done, bf16[]{:T(256)} %constant.134), dimensions={1}, to_apply=%all-gather.reduce_sub_computation | reduce | bytes 2097154 | tf_op jit(solution)/shard_map/all_gather | solution.py:231
  465.6 0.7 copy.81
  (109 shorter events, 10.0 us)
Async XLA Ops:
  7.2 21.4 %copy-start = (bf16[256,1024]{1,0:T(8,128)(2,1)S(1)}, bf16[256,1024]{1,0:T(8,128)(2,1)}, u32[]{:S(2)}) copy-start(bf16[256,1024]{1,0:T(8,128)(2,1)} %param.29) | copy-start | bytes 1572868
  7.2 17.3 %copy-start.3 = (bf16[1,4096,128]{2,1,0:T(8,128)(2,1)S(1)}, bf16[1,4096,128]{2,1,0:T(8,128)(2,1)}, u32[]{:S(2)}) copy-start(bf16[1,4096,128]{2,1,0:T(8,128)(2,1)} %param.21) | copy-start | bytes 3145732
  7.2 57.5 %reduce-scatter.4.cloned.1.call-start = ((), (), s32[]{:S(2)}) async-start(), calls=%async_computation.5 | async-start | bytes 327680 | tf_op jit(solution)/shard_map/reduce_scatter | solution.py:159
  26.6 3.0 copy-start.14
  26.6 4.0 copy-start.7
  28.1 36.7 %copy-start.2 = (bf16[1,32,1024]{2,1,0:T(8,128)(2,1)S(1)}, bf16[1,32,1024]{2,1,0:T(8,128)(2,1)}, u32[]{:S(2)}) copy-start(bf16[1,32,1024]{2,1,0:T(8,128)(2,1)} %param.20) | copy-start | bytes 196612
  28.1 37.6 %copy-start.10 = (f32[1024]{0:T(1024)S(1)}, f32[1024]{0:T(1024)}, u32[]{:S(2)}) copy-start(f32[1024]{0:T(1024)} %param.31) | copy-start | bytes 12292
  29.5 237.6 %reduce-scatter.6.cloned.1.call-start = ((), (), s32[]{:S(2)}) async-start(), calls=%async_computation.6 | async-start | bytes 3932160 | tf_op jit(solution)/shard_map/reduce_scatter | solution.py:201
  90.4 117.1 %copy-start.11 = (bf16[1,1024,128]{2,1,0:T(8,128)(2,1)S(1)}, bf16[1,1024,128]{2,1,0:T(8,128)(2,1)}, u32[]{:S(2)}) copy-start(bf16[1,1024,128]{2,1,0:T(8,128)(2,1)} %param.33) | copy-start | bytes 786436
  205.5 1.9 copy-start.1
  207.4 3.5 copy-start.12
  207.4 3.5 copy-start.13
  219.9 65.2 %copy-start.8 = (bf16[1024,32]{0,1:T(8,128)(2,1)S(1)}, bf16[1024,32]{0,1:T(8,128)(2,1)}, u32[]{:S(2)}) copy-start(bf16[1024,32]{0,1:T(8,128)(2,1)} %param.32) | copy-start | bytes 196612
  269.9 63.1 %copy-start.4 = (bf16[32,1024]{1,0:T(8,128)(2,1)S(1)}, bf16[32,1024]{1,0:T(8,128)(2,1)}, u32[]{:S(2)}) copy-start(bf16[32,1024]{1,0:T(8,128)(2,1)} %reduce-scatter.4.cloned.1.call-done) | copy-start | bytes 196612
  269.9 45.4 %all-to-all-start.1 = ((bf16[128,1,3,1024]{3,2,1,0:T(4,128)(2,1)}), bf16[128,1,3,1024]{3,2,1,0:T(4,128)(2,1)S(1)}, u32[]{:S(2)}, u32[]{:S(2)}) async-start(bf16[128,1,3,1024]{3,2,1,0:T(4,128)(2,1)} %copy.79), calls=%async_computation.3 | async-start | bytes 2097152 | tf_op jit(solution)/shard_map/all_to_all | solution.py:204
  284.4 48.6 %reduce-scatter.8.cloned.1.call-start = ((), (), s32[]{:S(2)}) async-start(), calls=%async_computation.7 | async-start | bytes 327680 | tf_op jit(solution)/shard_map/reduce_scatter | solution.py:223
  317.0 139.0 %all-gather.3.cloned.1.call-start = ((), (), s32[]{:S(2)}) async-start(), calls=%async_computation.8 | async-start | bytes 2101248 | tf_op jit(solution)/shard_map/all_gather | solution.py:231
  333.9 130.6 %copy-start.6 = (bf16[32,1024]{1,0:T(8,128)(2,1)}, bf16[32,1024]{1,0:T(8,128)(2,1)S(1)}, u32[]{:S(2)}) copy-start(bf16[32,1024]{1,0:T(8,128)(2,1)S(1)} %fusion.64) | copy-start | bytes 196612
  334.5 130.1 %copy-start.5 = (bf16[1024,96]{0,1:T(8,128)(2,1)S(1)}, bf16[1024,96]{0,1:T(8,128)(2,1)}, u32[]{:S(2)}) copy-start(bf16[1024,96]{0,1:T(8,128)(2,1)} %param.37) | copy-start | bytes 589828
  334.5 130.1 %copy-start.9 = (f32[1024]{0:T(1024)S(1)}, f32[1024]{0:T(1024)}, u32[]{:S(2)}) copy-start(f32[1024]{0:T(1024)} %param.36) | copy-start | bytes 12292
Sparse Core Ops, SparseCore 0:
  29.6 35.0 reduce-scatter.3
  220.0 47.0 reduce-scatter.5
  317.2 15.7 reduce-scatter.7
  337.6 118.3 all-gather.2
where the time goes:
time: 474 us; the launch traced here: 473 us
  waiting for transfers between devices  235 us (50%)
  blocking collectives  135 us (28%)
  local copies, waits for them, and re-layouts  38.4 us (8%)
  matrix products  17.4 us (4%)
  other arithmetic  17.1 us (4%)
  between operations  15 us (3%)
  starting transfers between devices  14.9 us (3%)
    all_gather x1, waiting for transfers between devices, body(): lax.all_gather(tail_row, ('req', 'tp'), axis=0, tiled=True)  121 us
    all_to_all x1, blocking collectives, body(): lax.all_to_all(outgoing, 'req', split_axis=0, concat_axis=0, tiled=True)  115 us
    reduce_scatter x1, waiting for transfers between devices, body(): lax.psum_scatter(partial_value.astype(jnp.bfloat16), 'tp', scatter_dimens...  47.2 us
    reduce_scatter x1, waiting for transfers between devices, body(): lax.psum_scatter(jnp.dot(attended, out_weight, preferred_element_type=jnp...  28.6 us
    all_to_all x1, waiting for transfers between devices, body(): lax.all_to_all(unit_sum, 'req', split_axis=0, concat_axis=0, tiled=True)  21.8 us
    reduce_scatter x1, waiting for transfers between devices, body(): lax.psum_scatter(jnp.dot(combine, flat_back, preferred_element_type=jnp.f...  15.9 us
    all_to_all x1, starting transfers between devices, body(): lax.all_to_all(unit_sum, 'req', split_axis=0, concat_axis=0, tiled=True)  14.5 us
    gather x2, local copies, waits for them, and re-layouts, body(): jnp.take(expert_rows, slot_token, axis=0, mode='fill', fill_value=0)  11.9 us
  transfers between devices with their start and end apart: 5, of which 5 were waited for; matrix products, arithmetic and copies ran while one was open for 3% of the time, Pallas kernels for 0%

commit v1 on v0

--- a/solution.py
+++ b/solution.py
@@ -1,5 +1,9 @@
+import functools
+
 import jax
 import jax.numpy as jnp
+from jax.experimental import pallas as pl
+from jax.experimental.pallas import tpu as pltpu
 from jax import lax
 from jax.sharding import PartitionSpec as P
 
@@ -7,6 +11,9 @@
 EXPERTS = 32
 TOPK = 8
 SPAN = 128
+SLOT_ROWS = 16
+MESH = pl.DeviceIdType.MESH
+VMEM_SPEC = pl.BlockSpec(memory_space=pltpu.VMEM)
 
 
 epsilon = 1e-06
@@ -77,6 +84,390 @@
         jnp.zeros((token_count, key_heads, group_size), jnp.float32),
     )
     return lax.fori_loop(first_block, last_block, block_step, initial)
+
+
+def send(source, target, send_sem, recv_sem, device):
+    return pltpu.make_async_remote_copy(
+        src_ref=source,
+        dst_ref=target,
+        send_sem=send_sem,
+        recv_sem=recv_sem,
+        device_id=device,
+        device_id_type=MESH,
+    )
+
+
+def greet(barrier, device):
+    pl.semaphore_signal(barrier, inc=1, device_id=device, device_id_type=MESH)
+
+
+def lane_gather_kernel(lanes, own_ref, all_ref, send_sem, recv_sem, local_sem):
+    req, me = lax.axis_index("req"), lax.axis_index("tp")
+    rows = own_ref.shape[0]
+    place = pl.ds(pl.multiple_of(me * rows, rows), rows)
+    barrier = pltpu.get_barrier_semaphore()
+    for step in range(1, lanes):
+        greet(barrier, (req, lax.rem(me + step, lanes)))
+    local = pltpu.make_async_copy(own_ref, all_ref.at[place], local_sem)
+    local.start()
+    pl.semaphore_wait(barrier, lanes - 1)
+    copies = []
+    for step in range(1, lanes):
+        copy = send(
+            own_ref,
+            all_ref.at[place],
+            send_sem.at[step - 1],
+            recv_sem.at[step - 1],
+            (req, lax.rem(me + step, lanes)),
+        )
+        copy.start()
+        copies.append(copy)
+    for copy in copies:
+        copy.wait()
+    local.wait()
+
+
+def lane_gather(own, lanes):
+    rows, width = own.shape
+    return pl.pallas_call(
+        functools.partial(lane_gather_kernel, lanes),
+        out_shape=jax.ShapeDtypeStruct((lanes * rows, width), own.dtype),
+        in_specs=[VMEM_SPEC],
+        out_specs=VMEM_SPEC,
+        scratch_shapes=[
+            pltpu.SemaphoreType.DMA((lanes - 1,)),
+            pltpu.SemaphoreType.DMA((lanes - 1,)),
+            pltpu.SemaphoreType.DMA,
+        ],
+        compiler_params=pltpu.CompilerParams(collective_id=0, has_side_effects=True),
+        name="lane_gather",
+    )(own)
+
+
+def mix_kernel(lanes, part_ref, own_ref, gain_ref, mixed_ref, expert_ref, held, send_sem, recv_sem):
+    req, me = lax.axis_index("req"), lax.axis_index("tp")
+    rows = own_ref.shape[0]
+    barrier = pltpu.get_barrier_semaphore()
+    for step in range(1, lanes):
+        greet(barrier, (req, lax.rem(me + step, lanes)))
+    pl.semaphore_wait(barrier, lanes - 1)
+    copies = []
+    for step in range(1, lanes):
+        other = lax.rem(me + step, lanes)
+        copy = send(
+            part_ref.at[pl.ds(pl.multiple_of(other * rows, rows), rows)],
+            held.at[step - 1],
+            send_sem.at[step - 1],
+            recv_sem.at[step - 1],
+            (req, other),
+        )
+        copy.start()
+        copies.append(copy)
+    total = part_ref[pl.ds(pl.multiple_of(me * rows, rows), rows), :].astype(jnp.float32)
+    for step, copy in enumerate(copies):
+        copy.wait()
+        total = total + held[step].astype(jnp.float32)
+    mixed = (own_ref[...].astype(jnp.float32) + total).astype(jnp.bfloat16)
+    mixed_ref[...] = mixed
+    expert_ref[...] = rms_scale(mixed, gain_ref[...]).astype(jnp.bfloat16)
+
+
+def mix_rows(partial_rows, own, gain, lanes):
+    rows, width = own.shape
+    return pl.pallas_call(
+        functools.partial(mix_kernel, lanes),
+        out_shape=[jax.ShapeDtypeStruct((rows, width), jnp.bfloat16)] * 2,
+        in_specs=[VMEM_SPEC] * 3,
+        out_specs=[VMEM_SPEC] * 2,
+        scratch_shapes=[
+            pltpu.VMEM((lanes - 1, rows, width), jnp.bfloat16),
+            pltpu.SemaphoreType.DMA((lanes - 1,)),
+            pltpu.SemaphoreType.DMA((lanes - 1,)),
+        ],
+        compiler_params=pltpu.CompilerParams(collective_id=1, has_side_effects=True),
+        name="mix_rows",
+    )(partial_rows, own, gain)
+
+
+def expert_kernel(
+    lanes,
+    copies_of,
+    group,
+    out_ref,
+    gate_ref,
+    up_ref,
+    down_ref,
+    back_ref,
+    arrived,
+    result,
+    gates,
+    ups,
+    downs,
+    go_send,
+    go_recv,
+    ret_send,
+    ret_recv,
+    weight_send,
+    weight_recv,
+    local_sem,
+):
+    req, me = lax.axis_index("req"), lax.axis_index("tp")
+    experts = out_ref.shape[0]
+    width = out_ref.shape[2]
+    mine, replica = req // copies_of, lax.rem(req, copies_of)
+    barrier = pltpu.get_barrier_semaphore()
+
+    def peer(step):
+        return (lax.rem(mine + step, experts) * copies_of + replica, me)
+
+    for step in range(1, lanes):
+        greet(barrier, (req, lax.rem(me + step, lanes)))
+
+    @pl.loop(1, experts)
+    def _(step):
+        greet(barrier, peer(step))
+
+    own_block = pltpu.make_async_copy(out_ref.at[mine], arrived.at[0], local_sem.at[0])
+    own_block.start()
+    pl.semaphore_wait(barrier, lanes - 1 + experts - 1)
+
+    def weight_copies():
+        found = []
+        for step in range(1, lanes):
+            for number, (source, target) in enumerate(
+                ((gate_ref, gates), (up_ref, ups), (down_ref, downs))
+            ):
+                found.append(
+                    send(
+                        source,
+                        target.at[step - 1],
+                        weight_send.at[step - 1, number],
+                        weight_recv.at[step - 1, number],
+                        (req, lax.rem(me + step, lanes)),
+                    )
+                )
+        return found
+
+    def go_copy(step):
+        return send(
+            out_ref.at[lax.rem(mine + step, experts)],
+            arrived.at[step],
+            go_send.at[step],
+            go_recv.at[step],
+            peer(step),
+        )
+
+    def return_copy(step):
+        return send(
+            result.at[step],
+            back_ref.at[mine],
+            ret_send.at[step],
+            ret_recv.at[step],
+            (lax.rem(mine + experts - step, experts) * copies_of + replica, me),
+        )
+
+    for copy in weight_copies():
+        copy.start()
+
+    @pl.loop(1, experts)
+    def _(step):
+        go_copy(step).start()
+
+    own_block.wait()
+    for copy in weight_copies():
+        copy.wait()
+
+    @pl.loop(0, experts // group)
+    def _(number):
+        first = number * group
+        for offset in range(group):
+            step = first + offset
+
+            @pl.when(step > 0)
+            def _():
+                go_copy(step).wait_recv()
+
+        rows = arrived[pl.ds(first, group)].reshape(group * SLOT_ROWS, width)
+        total = None
+        for lane in range(lanes):
+            gate_block = gate_ref[...] if lane == 0 else gates[lane - 1]
+            up_block = up_ref[...] if lane == 0 else ups[lane - 1]
+            down_block = down_ref[...] if lane == 0 else downs[lane - 1]
+            gate_part = jnp.dot(rows, gate_block, preferred_element_type=jnp.float32)
+            up_part = jnp.dot(rows, up_block, preferred_element_type=jnp.float32)
+            hidden = (gate_part / (1.0 + jnp.exp(-gate_part)) * up_part).astype(jnp.bfloat16)
+            term = jnp.dot(hidden, down_block, preferred_element_type=jnp.float32)
+            total = term if total is None else total + term
+        result[pl.ds(first, group)] = total.astype(jnp.bfloat16).reshape(group, SLOT_ROWS, width)
+        for offset in range(group):
+            step = first + offset
+
+            @pl.when(step > 0)
+            def _():
+                return_copy(step).start()
+
+            @pl.when(step == 0)
+            def _():
+                pltpu.make_async_copy(
+                    result.at[0], back_ref.at[mine], local_sem.at[1]
+                ).start()
+
+    pltpu.make_async_copy(result.at[0], back_ref.at[mine], local_sem.at[1]).wait()
+
+    @pl.loop(1, experts)
+    def _(step):
+        go_copy(step).wait_send()
+        return_copy(step).wait()
+
+
+def expert_exchange(outgoing, gate, up, down, lanes, copies_of):
+    experts, slot_rows, width = outgoing.shape
+    units = gate.shape[1]
+    held = pltpu.VMEM((experts, slot_rows, width), jnp.bfloat16)
+    return pl.pallas_call(
+        functools.partial(expert_kernel, lanes, copies_of, 8),
+        out_shape=jax.ShapeDtypeStruct((experts, slot_rows, width), jnp.bfloat16),
+        in_specs=[VMEM_SPEC] * 4,
+        out_specs=VMEM_SPEC,
+        scratch_shapes=[
+            held,
+            held,
+            pltpu.VMEM((lanes - 1, width, units), jnp.bfloat16),
+            pltpu.VMEM((lanes - 1, width, units), jnp.bfloat16),
+            pltpu.VMEM((lanes - 1, units, width), jnp.bfloat16),
+            pltpu.SemaphoreType.DMA((experts,)),
+            pltpu.SemaphoreType.DMA((experts,)),
+            pltpu.SemaphoreType.DMA((experts,)),
+            pltpu.SemaphoreType.DMA((experts,)),
+            pltpu.SemaphoreType.DMA((lanes - 1, 3)),
+            pltpu.SemaphoreType.DMA((lanes - 1, 3)),
+            pltpu.SemaphoreType.DMA((2,)),
+        ],
+        compiler_params=pltpu.CompilerParams(collective_id=2, has_side_effects=True),
+        name="expert_exchange",
+    )(outgoing, gate, up, down)
+
+
+def tail_kernel(
+    lanes,
+    near,
+    far,
+    tail_ref,
+    gain_ref,
+    order_ref,
+    vocab_ref,
+    logits_ref,
+    rows_ref,
+    lane_send,
+    lane_recv,
+    near_send,
+    near_recv,
+    far_send,
+    far_recv,
+    local_sem,
+):
+    req, me = lax.axis_index("req"), lax.axis_index("tp")
+    plane, place = req // near, lax.rem(req, near)
+    last = lanes - 1
+    barrier = pltpu.get_barrier_semaphore()
+    for step in range(1, lanes):
+        greet(barrier, (req, lax.rem(me + step, lanes)))
+    for step in range(1, near):
+        greet(barrier, (plane * near + lax.rem(place + step, near), me))
+    for step in range(1, far):
+        greet(barrier, (lax.rem(plane + step, far) * near + place, me))
+    pl.semaphore_wait(barrier, lanes - 1 + near - 1 + far - 1)
+
+    @pl.when(me == last)
+    def _():
+        own = pltpu.make_async_copy(tail_ref, rows_ref.at[req], local_sem)
+        own.start()
+        copies = [
+            send(tail_ref, rows_ref.at[req], lane_send.at[lane], lane_recv, (req, lane))
+            for lane in range(last)
+        ]
+        for copy in copies:
+            copy.start()
+        own.wait()
+        for copy in copies:
+            copy.wait_send()
+
+    @pl.when(me != last)
+    def _():
+        send(tail_ref, rows_ref.at[req], lane_send.at[0], lane_recv, (req, last)).wait_recv()
+
+    copies = []
+    for step in range(1, near):
+        copy = send(
+            rows_ref.at[req],
+            rows_ref.at[req],
+            near_send.at[step - 1],
+            near_recv.at[step - 1],
+            (plane * near + lax.rem(place + step, near), me),
+        )
+        copy.start()
+        copies.append(copy)
+    for copy in copies:
+        copy.wait()
+    copies = []
+    block = pl.ds(plane * near, near)
+    for step in range(1, far):
+        copy = send(
+            rows_ref.at[block],
+            rows_ref.at[block],
+            far_send.at[step - 1],
+            far_recv.at[step - 1],
+            (lax.rem(plane + step, far) * near + place, me),
+        )
+        copy.start()
+        copies.append(copy)
+    for copy in copies:
+        copy.wait()
+
+    count, parts, lanes_wide = rows_ref.shape
+    square = jnp.zeros((count, 1), jnp.float32)
+    for part in range(parts):
+        piece = rows_ref[:, part, :]
+        square = square + jnp.sum(piece * piece, axis=-1, keepdims=True)
+    scale = lax.rsqrt(square / (parts * lanes_wide) + epsilon)
+    chosen = (
+        lax.broadcasted_iota(jnp.int32, (count, count), 0) == order_ref[...]
+    ).astype(jnp.bfloat16)
+    total = jnp.zeros(logits_ref.shape, jnp.float32)
+    for part in range(parts):
+        final = (rows_ref[:, part, :] * scale * gain_ref[part, :][None, :]).astype(jnp.bfloat16)
+        ordered = jnp.dot(chosen, final, preferred_element_type=jnp.float32).astype(jnp.bfloat16)
+        total = total + jnp.dot(
+            ordered,
+            vocab_ref[part * lanes_wide : (part + 1) * lanes_wide, :],
+            preferred_element_type=jnp.float32,
+        )
+    logits_ref[...] = total
+
+
+def tail_logits(tail, gain, order, vocab, lanes):
+    reqs = order.shape[1]
+    near = 16 if reqs % 16 == 0 else reqs
+    far = reqs // near
+    parts, wide = tail.shape
+    return pl.pallas_call(
+        functools.partial(tail_kernel, lanes, near, far),
+        out_shape=jax.ShapeDtypeStruct((reqs, vocab.shape[1]), jnp.float32),
+        in_specs=[VMEM_SPEC] * 4,
+        out_specs=VMEM_SPEC,
+        scratch_shapes=[
+            pltpu.VMEM((reqs, parts, wide), jnp.float32),
+            pltpu.SemaphoreType.DMA((lanes - 1,)),
+            pltpu.SemaphoreType.DMA,
+            pltpu.SemaphoreType.DMA((near - 1,)),
+            pltpu.SemaphoreType.DMA((near - 1,)),
+            pltpu.SemaphoreType.DMA((far - 1,)),
+            pltpu.SemaphoreType.DMA((far - 1,)),
+            pltpu.SemaphoreType.DMA,
+        ],
+        compiler_params=pltpu.CompilerParams(collective_id=3, has_side_effects=True),
+        name="tail_logits",
+    )(tail, gain, order, vocab)
 
 
 def body(
@@ -113,7 +504,7 @@
     attn_in = rms_scale(own_rows, attention_gain).astype(jnp.bfloat16)
     joined = jnp.concatenate([query_weight, key_weight, value_weight], axis=1)
     projected = jnp.dot(
-        lax.all_gather(attn_in, "tp", axis=0, tiled=True),
+        lane_gather(attn_in, lane_count),
         joined,
         preferred_element_type=jnp.float32,
     )
@@ -156,89 +547,48 @@
     numerator = numerator + own_numer
     denominator = denominator + own_denom
     attended = (numerator / denominator[..., None]).astype(jnp.bfloat16).reshape(SPAN, query_width)
-    attention_sum = lax.psum_scatter(
-        jnp.dot(attended, out_weight, preferred_element_type=jnp.float32).astype(jnp.bfloat16),
-        "tp",
-        scatter_dimension=0,
-        tiled=True,
-    ).astype(jnp.float32)
-    mixed_rows = (own_rows.astype(jnp.float32) + attention_sum).astype(jnp.bfloat16)
-    expert_in = rms_scale(mixed_rows, expert_gain).astype(jnp.bfloat16)
-    expert_rows = lax.all_gather(expert_in, "tp", axis=0, tiled=True)
-    router_logits = jnp.dot(expert_rows, router_weight, preferred_element_type=jnp.float32)
-    route_ids = routes[0]
-    chosen = route_ids[:, :, None] == jnp.arange(EXPERTS, dtype=jnp.int32)
-    picked = jnp.sum(jnp.where(chosen, router_logits[:, None, :], 0.0), axis=-1)
-    gate_expo = jnp.exp(picked)
+    head_rows = jnp.dot(attended, out_weight, preferred_element_type=jnp.float32).astype(
+        jnp.bfloat16
+    )
+    mixed_rows, expert_in = mix_rows(
+        head_rows, own_rows, expert_gain.reshape(1, model_width), lane_count
+    )
+    router_logits = jnp.dot(expert_in, router_weight, preferred_element_type=jnp.float32)
+    route_ids = lax.dynamic_slice_in_dim(routes[0], lane_index * shard_rows, shard_rows, 0)
+    expert_range = jnp.arange(EXPERTS, dtype=jnp.int32)
+    named = jnp.any(route_ids[:, :, None] == expert_range, axis=1)
+    gate_expo = jnp.where(named, jnp.exp(router_logits), 0.0)
     gate_values = (gate_expo / jnp.sum(gate_expo, axis=-1, keepdims=True)).astype(jnp.bfloat16)
-    replicas = max(1, req_count // EXPERTS)
-    block_len = SPAN // replicas
-    capacity = 3 * block_len * TOPK // (2 * EXPERTS)
-    local_experts = gate_weight.shape[0]
-    share_size = capacity // lane_count
-    counts = jnp.sum(chosen.astype(jnp.int32), axis=1)
-    blocked = counts.reshape(replicas, block_len, EXPERTS)
-    rank_table = (jnp.cumsum(blocked, axis=1) - blocked).reshape(SPAN, EXPERTS)
-    rank_pick = jnp.sum(jnp.where(chosen, rank_table[:, None, :], 0), axis=-1)
-    block_id = token_range // block_len
-    slot_ids = ((route_ids * replicas + block_id[:, None]) * capacity + rank_pick).reshape(-1)
-    slot_total = req_count * local_experts * capacity
-    token_ids = jnp.repeat(token_range, TOPK)
-    slot_token = jnp.full((slot_total,), SPAN, jnp.int32).at[slot_ids].set(token_ids)
-    slot_gate = jnp.zeros((slot_total,), jnp.bfloat16).at[slot_ids].set(gate_values.reshape(-1))
-    outgoing = jnp.take(expert_rows, slot_token, axis=0, mode="fill", fill_value=0).reshape(
-        req_count, local_experts, capacity, model_width
-    )
-    arrived = lax.all_to_all(outgoing, "req", split_axis=0, concat_axis=0, tiled=True)
-    gate_part = jnp.einsum(
-        "necd,edf->necf", arrived, gate_weight, preferred_element_type=jnp.float32
-    )
-    up_part = jnp.einsum("necd,edf->necf", arrived, up_weight, preferred_element_type=jnp.float32)
-    unit_hidden = (jax.nn.silu(gate_part) * up_part).astype(jnp.bfloat16)
-    partial_value = jnp.einsum(
-        "necf,efd->necd", unit_hidden, down_weight, preferred_element_type=jnp.float32
-    )
-    unit_sum = lax.psum_scatter(
-        partial_value.astype(jnp.bfloat16), "tp", scatter_dimension=2, tiled=True
-    )
-    returned = lax.all_to_all(unit_sum, "req", split_axis=0, concat_axis=0, tiled=True)
-    lane_tokens = lax.dynamic_slice_in_dim(
-        slot_token.reshape(req_count, local_experts, capacity),
-        lane_index * share_size,
-        share_size,
-        2,
-    ).reshape(-1)
-    lane_gates = lax.dynamic_slice_in_dim(
-        slot_gate.reshape(req_count, local_experts, capacity),
-        lane_index * share_size,
-        share_size,
-        2,
-    ).reshape(-1)
-    combine = jnp.where(
-        lane_tokens[None, :] == token_range[:, None],
-        lane_gates[None, :],
-        jnp.zeros((), jnp.bfloat16),
-    )
-    flat_back = returned.reshape(-1, model_width)
-    expert_sum = lax.psum_scatter(
-        jnp.dot(combine, flat_back, preferred_element_type=jnp.float32).astype(jnp.bfloat16),
-        "tp",
-        scatter_dimension=0,
-        tiled=True,
-    ).astype(jnp.float32)
+    counts = named.astype(jnp.int32)
+    ranks = jnp.where(named, jnp.cumsum(counts, axis=0) - 1, -1)
+    place = ranks.T[:, None, :] == jnp.arange(SLOT_ROWS, dtype=jnp.int32)[None, :, None]
+    picker = place.astype(jnp.bfloat16).reshape(EXPERTS * SLOT_ROWS, shard_rows)
+    combine = jnp.where(place, gate_values.T[:, None, :], jnp.zeros((), jnp.bfloat16)).reshape(
+        EXPERTS * SLOT_ROWS, shard_rows
+    )
+    outgoing = (
+        jnp.dot(picker, expert_in, preferred_element_type=jnp.float32)
+        .astype(jnp.bfloat16)
+        .reshape(EXPERTS, SLOT_ROWS, model_width)
+    )
+    returned = expert_exchange(
+        outgoing, gate_weight[0], up_weight[0], down_weight[0], lane_count, req_count // EXPERTS
+    )
+    expert_sum = lax.dot_general(
+        combine,
+        returned.reshape(EXPERTS * SLOT_ROWS, model_width),
+        (((0,), (0,)), ((), ())),
+        preferred_element_type=jnp.float32,
+    )
     layer_rows = (mixed_rows.astype(jnp.float32) + expert_sum).astype(jnp.bfloat16)
-    tail_row = layer_rows[shard_rows - 1 :]
-    every_tail = lax.all_gather(tail_row, ("req", "tp"), axis=0, tiled=True).reshape(
-        req_count, lane_count, model_width
-    )[:, lane_count - 1]
-    final_in = rms_scale(every_tail, final_gain).astype(jnp.bfloat16)
-    slot_logits = jnp.dot(final_in, vocab_weight, preferred_element_type=jnp.float32)
-    inverse = (
-        jnp.zeros((req_count,), jnp.int32)
-        .at[request_order]
-        .set(jnp.arange(req_count, dtype=jnp.int32))
-    )
-    logits = jnp.take(slot_logits, inverse, axis=0)
+    tail_row = layer_rows[shard_rows - 1].astype(jnp.float32).reshape(model_width // 128, 128)
+    logits = tail_logits(
+        tail_row,
+        final_gain.reshape(model_width // 128, 128),
+        request_order.reshape(1, req_count),
+        vocab_weight,
+        lane_count,
+    )
     return (layer_rows[None], logits)
 
 

time: 474 us -> 176 us (0.37)
  waiting for transfers between devices: 235 us -> 0 us
  Pallas kernels: 0 us -> 153 us
  blocking collectives: 135 us -> 0 us
  local copies, waits for them, and re-layouts: 38.4 us -> 6.55 us
  starting transfers between devices: 14.9 us -> 0 us
  between operations: 15 us -> 1.59 us
  other arithmetic: 17.1 us -> 4.98 us
  matrix products: 17.4 us -> 8.55 us
    pallas_call x0 -> x4, Pallas kernels: none -> 153 us  [the longest x1 87.4 us: expert_exchange(): pl.pallas_call(functools.partial(expert_kernel, lanes, copies_of, 8), out...]
    all_gather x1 -> x0, waiting for transfers between devices: 121 us -> none  [body(): lax.all_gather(tail_row, ('req', 'tp'), axis=0, tiled=True)]
    all_to_all x1 -> x0, blocking collectives: 115 us -> none  [body(): lax.all_to_all(outgoing, 'req', split_axis=0, concat_axis=0, tiled=True)]
    reduce_scatter x3 -> x0, waiting for transfers between devices: 91.7 us -> none  [the longest x1 47.2 us: body(): lax.psum_scatter(partial_value.astype(jnp.bfloat16), 'tp', scatter_dimens...]
    all_to_all x1 -> x0, waiting for transfers between devices: 21.8 us -> none  [body(): lax.all_to_all(unit_sum, 'req', split_axis=0, concat_axis=0, tiled=True)]
    all_gather x2 -> x0, blocking collectives: 19.9 us -> none  [the longest x1 10.5 us: body(): lax.all_gather(attn_in, 'tp', axis=0, tiled=True)]
    all_to_all x1 -> x0, starting transfers between devices: 14.5 us -> none  [body(): lax.all_to_all(unit_sum, 'req', split_axis=0, concat_axis=0, tiled=True)]
    scatter x3 -> x0, local copies, waits for them, and re-layouts: 12.9 us -> none  [the longest x1 7.59 us: body(): jnp.zeros((slot_total,), jnp.bfloat16).at[slot_ids]]
  transfers between devices with their start and end apart: 5 -> 0, of which waited for: 5 -> 0; matrix products, arithmetic and copies ran while one was open for 3% -> 0% of each run, Pallas kernels for 0% -> 0%
where the time goes in v1:
time: 176 us; the launch traced here: 175 us
  Pallas kernels  153 us (87%)
  matrix products  8.55 us (5%)
  local copies, waits for them, and re-layouts  6.55 us (4%)
  other arithmetic  4.98 us (3%)
    pallas_call x1, Pallas kernels, expert_exchange(): pl.pallas_call(functools.partial(expert_kernel, lanes, copies_of, 8), out...  87.4 us
    pallas_call x1, Pallas kernels, tail_logits(): pl.pallas_call(functools.partial(tail_kernel, lanes, near, far), out_shap...  48.9 us
    pallas_call x1, Pallas kernels, lane_gather(): pl.pallas_call(functools.partial(lane_gather_kernel, lanes), out_shape=ja...  9.12 us
    pallas_call x1, Pallas kernels, mix_rows(): pl.pallas_call(functools.partial(mix_kernel, lanes), out_shape=[jax.Shape...  7.81 us
    unnamed x18, local copies, waits for them, and re-layouts  4.44 us

profile of v1, /device:TPU:1, one launch (start us, length us, event | category | flops | bytes accessed | tf_op | source)
XLA Modules:
  0.0 174.9 jit_solution(10234051318129467287)
XLA Ops:
  0.7 1.4 dynamic_slice.12
  2.7 0.6 add_convert_fusion.2
  3.3 0.1 multiply_cosine_fusion
  3.4 1.0 fusion.24
  4.4 1.6 fusion.26.own_ref
  6.0 9.1 %lane_gather.1 = bf16[128,1024]{1,0:T(8,128)(2,1)} custom-call(bf16[32,1024]{1,0:T(8,128)(2,1)} %fusion.26.own_ref), custom_call_target="tpu_custom_call" | custom-call | tf_op jit(solution)/shard_map/lane_gather/pallas_call | solution.py:132
  15.1 1.7 fusion.17
  16.8 0.1 copy.55
  17.0 0.5 copy.57
  17.5 1.5 copy.58
  19.0 1.4 while.12
  19.1 0.6 fusion.67
  19.7 0.5 fusion.68
  20.2 0.2 fusion.69
  20.5 0.1 copy.54
  20.6 0.3 fusion.40
  20.9 0.1 copy.53
  21.0 0.2 fusion.15
  21.2 0.9 convolution_convert_fusion.1.part_ref
  22.2 7.8 %mix_rows.1 = (bf16[32,1024]{1,0:T(8,128)(2,1)}, bf16[32,1024]{1,0:T(8,128)(2,1)}) custom-call(bf16[128,1024]{1,0:T(8,128)(2,1)} %convolution_convert_fusion.1.part_ref, bf16[32,1024]{1,0:T(8,128)(2,1)} %bitcast.107, f32[1,1024]{1,0:T(1,128)} %bitcast.122), custom_call_target="tpu_custom_call" | custom-call | tf_op jit(solution)/shard_map/mix_rows/pallas_call | solution.py:177
  30.1 0.1 fusion.30
  30.3 0.1 copy.61
  30.4 1.0 fusion.41
  31.5 0.1 eq.48
  31.6 0.1 bitcast_compare_fusion
  31.8 2.2 %convolution_convert_fusion = bf16[512,1024]{1,0:T(8,128)(2,1)} fusion(pred[512,32]{1,0:T(32,128)(4,1)S(1)} %bitcast_compare_fusion, bf16[32,1024]{1,0:T(8,128)(2,1)} %get-tuple-element.51), kind=kOutput, calls=%fused_computation.13 | convolution fusion | flops 34078720 | bytes 1130496 | tf_op jit(solution)/shard_map/dot_general | solution.py:570
  34.0 87.4 %expert_exchange.1 = bf16[32,16,1024]{2,1,0:T(8,128)(2,1)} custom-call(bf16[32,16,1024]{2,1,0:T(8,128)(2,1)} %bitcast.103, bf16[1024,128]{1,0:T(8,128)(2,1)} %bitcast.110, bf16[1024,128]{1,0:T(8,128)(2,1)} %bitcast.111, bf16[128,1024]{1,0:T(8,128)(2,1)} %bitcast.112), custom_call_target="tpu_custom_call" | custom-call | tf_op jit(solution)/shard_map/expert_exchange/pallas_call | solution.py:327
  121.4 1.6 fusion.14
  123.0 0.6 slice_convert_fusion.1
  123.6 0.8 copy.62.vocab_ref
  124.5 48.9 %tail_logits.1 = f32[128,96]{1,0:T(8,128)} custom-call(f32[8,128]{1,0:T(8,128)} %bitcast.120, f32[8,128]{1,0:T(8,128)} %bitcast.121, s32[1,128]{1,0:T(1,128)} %bitcast.123, bf16[1024,96]{1,0:T(8,128)(2,1)} %copy.62.vocab_ref), custom_call_target="tpu_custom_call" | custom-call | tf_op jit(solution)/shard_map/tail_logits/pallas_call | solution.py:453
  173.3 1.6 copy.63
  (36 shorter events, 0.5 us)
Async XLA Ops:
  0.6 20.6 %copy-start = (bf16[256,1024]{1,0:T(8,128)(2,1)S(1)}, bf16[256,1024]{1,0:T(8,128)(2,1)}, u32[]{:S(2)}) copy-start(bf16[256,1024]{1,0:T(8,128)(2,1)} %param.29) | copy-start | bytes 1572868
  15.1 1.9 %copy-start.1 = (bf16[1,4096,128]{2,1,0:T(8,128)(2,1)S(1)}, bf16[1,4096,128]{2,1,0:T(8,128)(2,1)}, u32[]{:S(2)}) copy-start(bf16[1,4096,128]{2,1,0:T(8,128)(2,1)} %param.22) | copy-start | bytes 3145732
  20.9 9.1 %copy-start.6 = (s32[1,128,8]{1,2,0:T(8,128)S(1)}, s32[1,128,8]{1,2,0:T(8,128)}, u32[]{:S(2)}) copy-start(s32[1,128,8]{1,2,0:T(8,128)} %param.25) | copy-start | bytes 12292
  20.9 9.5 %copy-start.5 = (bf16[1024,32]{0,1:T(8,128)(2,1)S(1)}, bf16[1024,32]{0,1:T(8,128)(2,1)}, u32[]{:S(2)}) copy-start(bf16[1024,32]{0,1:T(8,128)(2,1)} %param.32) | copy-start | bytes 196612
  34.0 87.4 %copy-start.4 = (bf16[32,1024]{1,0:T(8,128)(2,1)S(1)}, bf16[32,1024]{1,0:T(8,128)(2,1)}, u32[]{:S(2)}) copy-start(bf16[32,1024]{1,0:T(8,128)(2,1)} %get-tuple-element.50) | copy-start | bytes 196612
  121.4 2.2 %copy-start.2 = (bf16[1024,96]{0,1:T(8,128)(2,1)S(1)}, bf16[1024,96]{0,1:T(8,128)(2,1)}, u32[]{:S(2)}) copy-start(bf16[1024,96]{0,1:T(8,128)(2,1)} %param.37) | copy-start | bytes 589828
  123.0 51.9 %copy-start.3 = (bf16[32,1024]{1,0:T(8,128)(2,1)}, bf16[32,1024]{1,0:T(8,128)(2,1)S(1)}, u32[]{:S(2)}) copy-start(bf16[32,1024]{1,0:T(8,128)(2,1)S(1)} %fusion.14) | copy-start | bytes 196612

commit v2 on v0

v2 whole, which is shorter than its diff:
```python
import jax
import jax.numpy as jnp
from jax.experimental import pallas as pl
from jax.experimental.pallas import tpu as pltpu
from jax import lax
from jax.sharding import PartitionSpec as P

HEAD_DIM = 64
EXPERTS = 32
TOPK = 8
LANES = 4
RING_Y = 8
RING_Z = 8
SPAN = 128
SLOT_ROWS = 16
CAP = 12
PACKED = 768
CHUNK = 256
MESH = pl.DeviceIdType.MESH
VMEM_SPEC = pl.BlockSpec(memory_space=pltpu.VMEM)


epsilon = 1e-06
key_block = 512
float32 = jnp.float32
bfloat16 = jnp.bfloat16


def rms_scale(row_block, gain_vector):
    widened = row_block.astype(jnp.float32)
    return (
        widened
        * lax.rsqrt(jnp.mean(widened * widened, axis=-1, keepdims=True) + epsilon)
        * gain_vector
    )


def send(source, target, send_sem, recv_sem, device):
    return pltpu.make_async_remote_copy(
        src_ref=source,
        dst_ref=target,
        send_sem=send_sem,
        recv_sem=recv_sem,
        device_id=device,
        device_id_type=MESH,
    )


def greet(barrier, device):
    pl.semaphore_signal(barrier, inc=1, device_id=device, device_id_type=MESH)


def dot(a, b):
    return jnp.dot(a, b, preferred_element_type=float32)


def dot_last(a, b):
    return lax.dot_general(a, b, (((1,), (1,)), ((), ())), preferred_element_type=float32)


def iota(shape, axis):
    return lax.broadcasted_iota(jnp.int32, shape, axis)


def one_hot(mask):
    return jnp.where(mask, 1.0, 0.0).astype(bfloat16)


def packed_rank(slot_row, chunk):
    if chunk is None:
        return jnp.where(slot_row < CAP, slot_row, -1)
    return jnp.where(slot_row >= CAP, slot_row - CAP + (SLOT_ROWS - CAP) * chunk, -1)


def layer_kernel(
    length_ref,
    own_ref,
    keys_ref,
    values_ref,
    table_ref,
    routes_ref,
    query_ref,
    key_ref,
    value_ref,
    out_ref,
    attention_gain_ref,
    expert_gain_ref,
    router_ref,
    gate_ref,
    up_ref,
    down_ref,
    final_gain_ref,
    order_ref,
    vocab_ref,
    layer_ref,
    logits_ref,
    normed,
    all_rows,
    stacked,
    numerator,
    denominator,
    part,
    part_held,
    outgoing,
    arrived,
    result,
    back,
    gates,
    ups,
    downs,
    tail,
    tails,
    tails_wide,
    row_send,
    row_recv,
    mix_send,
    mix_recv,
    weight_send,
    weight_recv,
    go_send,
    go_recv,
    ret_send,
    ret_recv,
    lane_send,
    lane_recv,
    plane_send,
    plane_recv,
    core_sem,
    local_sem,
):
    req, me = lax.axis_index("req"), lax.axis_index("tp")
    z, y, core = req // (2 * RING_Y), lax.rem(req // 2, RING_Y), lax.rem(req, 2)
    place = req // 2
    places = RING_Y * RING_Z
    mine = place // 2
    experts, _, _ = outgoing.shape
    rows, width = own_ref.shape
    partner = z * 2 * RING_Y + y * 2 + 1 - core
    last = LANES - 1
    barrier = pltpu.get_barrier_semaphore()

    def lane(step):
        return (req, lax.rem(me + step, LANES))

    def plane_peer(step):
        return (lax.rem(place + step, places) * 2 + core, me)

    for step in range(1, LANES):
        greet(barrier, lane(step))
    greet(barrier, (partner, me))

    @pl.loop(1, places)
    def _(step):
        greet(barrier, plane_peer(step))

    normed[...] = rms_scale(own_ref[...], attention_gain_ref[...]).astype(bfloat16)
    own_place = pl.ds(pl.multiple_of(me * rows, rows), rows)
    local = pltpu.make_async_copy(normed, all_rows.at[own_place], local_sem.at[0])
    local.start()
    pl.semaphore_wait(barrier, LANES - 1 + 1 + places - 1)

    row_copies = [
        send(normed, all_rows.at[own_place], row_send.at[step - 1], row_recv.at[step - 1], lane(step))
        for step in range(1, LANES)
    ]
    for copy in row_copies:
        copy.start()
    triples = ((gate_ref, gates), (up_ref, ups), (down_ref, downs))

    def near_weights():
        return [
            send(
                source,
                target.at[side],
                weight_send.at[side, number],
                weight_recv.at[side, number],
                lane((1, LANES - 1)[side]),
            )
            for number, (source, target) in enumerate(triples)
            for side in range(2)
        ]

    def far_weights():
        found = []
        for number, (source, target) in enumerate(triples):
            half = source.shape[0] // 2
            for side in range(2):
                piece = pl.ds(side * half, half)
                found.append(
                    send(
                        target.at[side, piece],
                        target.at[2, piece],
                        weight_send.at[2 + side, number],
                        weight_recv.at[2 + side, number],
                        lane((1, LANES - 1)[side]),
                    )
                )
        return found

    for copy in near_weights():
        copy.start()
    for copy in row_copies:
        copy.wait()
    local.wait()

    lanes_at = iota((SPAN, 128), 1)
    front = lax.rem(lanes_at, HEAD_DIM) < HEAD_DIM // 2
    first_head = lanes_at < HEAD_DIM
    cosine, sine = table_ref[0], table_ref[1]
    token_rows = all_rows[...]

    def turned(piece):
        other = jnp.where(
            front, -pltpu.roll(piece, 128 - HEAD_DIM // 2, 1), pltpu.roll(piece, HEAD_DIM // 2, 1)
        )
        return piece * cosine + other * sine

    projected = dot(token_rows, query_ref[...])
    zero = jnp.zeros((SPAN, 128), float32)
    for group in range(2):
        piece = turned(projected[:, group * 128 : (group + 1) * 128]).astype(bfloat16).astype(float32)
        piece = piece * HEAD_DIM ** (-0.5)
        swapped = pltpu.roll(piece, HEAD_DIM, 1)
        keep = first_head if group == 0 else jnp.logical_not(first_head)
        pair = (piece, swapped) if group == 0 else (swapped, piece)
        for member in range(2):
            at = (group * 2 + member) * SPAN
            stacked[at : at + SPAN, :] = jnp.where(keep, pair[member], zero).astype(bfloat16)
    new_keys = turned(dot(token_rows, key_ref[...])).astype(bfloat16)
    new_values = dot(token_rows, value_ref[...]).astype(bfloat16)
    heads = 4 * SPAN
    causal = iota((heads, SPAN), 1) <= lax.rem(iota((heads, SPAN), 0), SPAN)
    expo = jnp.where(causal, jnp.exp(dot_last(stacked[...], new_keys)), 0.0)
    numerator[...] = dot(expo.astype(bfloat16), new_values)
    denominator[...] = jnp.sum(expo, axis=-1, keepdims=True)
    length = length_ref[req]

    @pl.loop(0, keys_ref.shape[0] // key_block)
    def _(number):
        at = pl.ds(pl.multiple_of(number * key_block, key_block), key_block)
        scores = dot_last(stacked[...], keys_ref[at, :])
        inside = iota((heads, key_block), 1) < length - number * key_block
        block = jnp.where(inside, jnp.exp(scores), 0.0)
        numerator[...] += dot(block.astype(bfloat16), values_ref[at, :])
        denominator[...] += jnp.sum(block, axis=-1, keepdims=True)

    mean_values = numerator[...] / denominator[...]
    head = [mean_values[at * SPAN : (at + 1) * SPAN] for at in range(4)]
    attended = jnp.concatenate(
        [
            jnp.where(first_head, head[0], pltpu.roll(head[1], HEAD_DIM, 1)),
            jnp.where(first_head, pltpu.roll(head[2], HEAD_DIM, 1), head[3]),
        ],
        axis=1,
    ).astype(bfloat16)
    part[...] = dot(attended, out_ref[...]).astype(bfloat16)

    mix_copies = []
    for step in range(1, LANES):
        other = lax.rem(me + step, LANES)
        mix_copies.append(
            send(
                part.at[pl.ds(pl.multiple_of(other * rows, rows), rows)],
                part_held.at[step - 1],
                mix_send.at[step - 1],
                mix_recv.at[step - 1],
                (req, other),
            )
        )
    for copy in mix_copies:
        copy.start()
    for copy in near_weights():
        copy.wait()
    for copy in far_weights():
        copy.start()
    total = part[own_place, :].astype(float32)
    for step, copy in enumerate(mix_copies):
        copy.wait()
        total = total + part_held[step].astype(float32)
    mixed = (own_ref[...].astype(float32) + total).astype(bfloat16)
    expert_in = rms_scale(mixed, expert_gain_ref[...]).astype(bfloat16)

    expert_at = iota((rows, EXPERTS), 1)
    named = jnp.zeros((rows, EXPERTS), float32)
    for choice in range(TOPK):
        named = named + jnp.where(routes_ref[:, choice : choice + 1] == expert_at, 1.0, 0.0)
    gate_expo = jnp.where(named > 0.0, jnp.exp(dot(expert_in, router_ref[...])), 0.0)
    gate_values = (gate_expo / jnp.sum(gate_expo, axis=-1, keepdims=True)).astype(bfloat16)
    earlier = one_hot(iota((rows, rows), 1) < iota((rows, rows), 0))
    ranks = jnp.where(named > 0.0, dot(earlier, named.astype(bfloat16)), 99.0).astype(bfloat16)
    slots = EXPERTS * SLOT_ROWS
    spread = one_hot(iota((slots, EXPERTS), 0) // SLOT_ROWS == iota((slots, EXPERTS), 1))
    slot_rank = dot_last(spread, ranks)
    slot_row = lax.rem(iota((slots, rows), 0), SLOT_ROWS)
    chunks = PACKED // CHUNK

    def picker(chunk):
        return one_hot(slot_rank == packed_rank(slot_row, chunk).astype(float32))

    main = picker(None)
    for chunk in range(chunks):
        span = slice(chunk * CHUNK, (chunk + 1) * CHUNK)
        piece = dot(main, expert_in[:, span]) + dot(picker(chunk), expert_in[:, PACKED:])
        outgoing[:, :, span] = piece.astype(bfloat16).reshape(EXPERTS, SLOT_ROWS, CHUNK)

    def target(step):
        far, near = step // 4, lax.rem(step, 4)
        to_z = lax.rem(z + far, RING_Z)
        sign = 1 - 2 * lax.rem(y + near, 2)
        to_y = lax.rem(y + sign * near + RING_Y, RING_Y)
        return to_z * RING_Y + to_y

    def origin(step):
        far, near = step // 4, lax.rem(step, 4)
        from_z = lax.rem(z - far + RING_Z, RING_Z)
        sign = 1 - 2 * lax.rem(y, 2)
        from_y = lax.rem(y - sign * near + RING_Y, RING_Y)
        return from_z * RING_Y + from_y

    def go_copy(step):
        to = target(step)
        return send(
            outgoing.at[to // 2], arrived.at[step], go_send.at[step], go_recv.at[step], (to * 2 + core, me)
        )

    def return_copy(step):
        return send(
            result.at[step],
            back.at[mine],
            ret_send.at[step],
            ret_recv.at[step],
            (origin(step) * 2 + core, me),
        )

    own_block = pltpu.make_async_copy(outgoing.at[mine], arrived.at[0], local_sem.at[1])
    own_block.start()

    @pl.loop(1, experts)
    def _(step):
        go_copy(step).start()

    own_block.wait()
    for copy in far_weights():
        copy.wait()

    group = 8
    group_rows = group * SLOT_ROWS
    row_at, column_at = iota((group_rows, group_rows), 0), iota((group_rows, group_rows), 1)
    same_slot = row_at // SLOT_ROWS == column_at // SLOT_ROWS
    row_in, column_in = lax.rem(row_at, SLOT_ROWS), lax.rem(column_at, SLOT_ROWS)
    kept = one_hot(same_slot & (packed_rank(row_in, None) == column_in))
    packs = [one_hot(same_slot & (packed_rank(row_in, chunk) == column_in)) for chunk in range(chunks)]
    unpacks = [one_hot(same_slot & (packed_rank(column_in, chunk) == row_in)) for chunk in range(chunks)]

    @pl.loop(0, experts // group)
    def _(number):
        first = number * group
        for offset in range(group):
            step = first + offset

            @pl.when(step > 0)
            def _():
                go_copy(step).wait_recv()

        block = arrived[pl.ds(first, group)].reshape(group_rows, PACKED)
        end = None
        for chunk in range(chunks):
            moved = dot(unpacks[chunk], block[:, chunk * CHUNK : (chunk + 1) * CHUNK])
            end = moved if end is None else end + moved
        whole = jnp.concatenate([block, end.astype(bfloat16)], axis=1)
        total = None
        for held in range(LANES):
            gate_block = gate_ref[...] if held == 0 else gates[held - 1]
            up_block = up_ref[...] if held == 0 else ups[held - 1]
            down_block = down_ref[...] if held == 0 else downs[held - 1]
            gate_part = dot(whole, gate_block)
            up_part = dot(whole, up_block)
            hidden = (gate_part / (1.0 + jnp.exp(-gate_part)) * up_part).astype(bfloat16)
            term = dot(hidden, down_block)
            total = term if total is None else total + term
        rounded = total.astype(bfloat16)
        for chunk in range(chunks):
            span = slice(chunk * CHUNK, (chunk + 1) * CHUNK)
            piece = dot(kept, rounded[:, span]) + dot(packs[chunk], rounded[:, PACKED:])
            result[pl.ds(first, group), :, span] = piece.astype(bfloat16).reshape(
                group, SLOT_ROWS, CHUNK
            )
        for offset in range(group):
            step = first + offset

            @pl.when(step > 0)
            def _():
                return_copy(step).start()

    own_back = pltpu.make_async_copy(result.at[0], back.at[mine], local_sem.at[2])
    own_back.start()
    wide_spread = one_hot(iota((EXPERTS, slots), 1) // SLOT_ROWS == iota((EXPERTS, slots), 0))
    row_rank = dot(ranks, wide_spread)
    row_gate = dot(gate_values, wide_spread)
    slot_column = lax.rem(iota((rows, slots), 1), SLOT_ROWS)

    def combine(chunk):
        found = row_rank == packed_rank(slot_column, chunk).astype(float32)
        return jnp.where(found, row_gate, 0.0).astype(bfloat16)

    main = combine(None)
    ends = [combine(chunk) for chunk in range(chunks)]
    own_back.wait()

    @pl.loop(1, experts)
    def _(step):
        return_copy(step).wait_recv()

    end = None
    sums = []
    for chunk in range(chunks):
        piece = back[:, :, chunk * CHUNK : (chunk + 1) * CHUNK].reshape(slots, CHUNK)
        sums.append(dot(main, piece))
        moved = dot(ends[chunk], piece)
        end = moved if end is None else end + moved
    sums.append(end)
    layer = (mixed.astype(float32) + jnp.concatenate(sums, axis=1)).astype(bfloat16)
    layer_ref[...] = layer
    parts = width // 128
    closing = layer[rows - 8 :, :].astype(float32)
    tail[...] = jnp.concatenate(
        [closing[7:8, at * 128 : (at + 1) * 128] for at in range(parts)], axis=0
    ).astype(bfloat16)

    def lane_copy(to):
        return send(tail, tails.at[core, place], lane_send.at[to], lane_recv, (req, to))

    @pl.when(me == last)
    def _():
        for to in range(last):
            lane_copy(to).start()
        own = pltpu.make_async_copy(tail, tails.at[core, place], local_sem.at[3])
        own.start()
        own.wait()
        for to in range(last):
            lane_copy(to).wait_send()

    @pl.when(me != last)
    def _():
        send(tail, tails.at[core, place], lane_send.at[0], lane_recv, (req, last)).wait_recv()

    def plane_copy(step):
        own_row = tails.at[core, place]
        return send(own_row, own_row, plane_send.at[step], plane_recv.at[step], plane_peer(step))

    @pl.loop(1, places)
    def _(step):
        plane_copy(step).start()

    @pl.loop(1, experts)
    def _(step):
        go_copy(step).wait_send()
        return_copy(step).wait_send()

    @pl.loop(1, places)
    def _(step):
        plane_copy(step).wait()

    half = send(tails.at[core], tails.at[core], core_sem.at[0], core_sem.at[1], (partner, me))
    half.start()
    half.wait()

    count = 2 * places
    tails_wide[...] = tails[...].astype(float32).reshape(count, parts, 128)
    square = jnp.zeros((count, 1), float32)
    for at in range(parts):
        piece = tails_wide[:, at, :]
        square = square + jnp.sum(piece * piece, axis=-1, keepdims=True)
    scale = lax.rsqrt(square / width + epsilon)
    chosen = one_hot(iota((count, count), 0) == order_ref[...])
    found = jnp.zeros(logits_ref.shape, float32)
    for at in range(parts):
        span = slice(at * 128, (at + 1) * 128)
        final = (tails_wide[:, at, :] * scale * final_gain_ref[:, span]).astype(bfloat16)
        ordered = dot(chosen, final).astype(bfloat16)
        found = found + dot(ordered, vocab_ref[span, :])
    logits_ref[...] = found


def body(
    hidden_in,
    cache_keys,
    cache_values,
    lengths,
    request_order,
    routes,
    query_weight,
    key_weight,
    value_weight,
    out_weight,
    attention_gain,
    expert_gain,
    router_weight,
    gate_weight,
    up_weight,
    down_weight,
    final_gain,
    vocab_weight,
):
    own_rows = hidden_in[0]
    rows, width = own_rows.shape
    units = gate_weight.shape[2]
    reqs = lengths.shape[0]
    places = reqs // 2
    half_dim = HEAD_DIM // 2
    frequency = jnp.exp(
        -jnp.log(10000.0) * jnp.arange(half_dim, dtype=float32) * (2.0 / HEAD_DIM)
    )
    positions = lengths[lax.axis_index("req")] + jnp.arange(SPAN, dtype=jnp.int32)
    angles = positions.astype(float32)[:, None] * jnp.tile(frequency, 128 // half_dim)[None, :]
    table = jnp.stack([jnp.cos(angles), jnp.sin(angles)])
    lane_routes = lax.dynamic_slice_in_dim(routes[0], lax.axis_index("tp") * rows, rows, 0)
    order = request_order.reshape(places, 2).T.reshape(1, reqs)
    dma = pltpu.SemaphoreType.DMA
    heads = 4 * SPAN
    slot_block = pltpu.VMEM((EXPERTS, SLOT_ROWS, PACKED), bfloat16)
    layer_rows, logits = pl.pallas_call(
        layer_kernel,
        out_shape=[
            jax.ShapeDtypeStruct((rows, width), bfloat16),
            jax.ShapeDtypeStruct((reqs, vocab_weight.shape[1]), float32),
        ],
        in_specs=[pl.BlockSpec(memory_space=pltpu.SMEM)] + [VMEM_SPEC] * 18,
        out_specs=[VMEM_SPEC] * 2,
        scratch_shapes=[
            pltpu.VMEM((rows, width), bfloat16),
            pltpu.VMEM((SPAN, width), bfloat16),
            pltpu.VMEM((heads, 128), bfloat16),
            pltpu.VMEM((heads, 128), float32),
            pltpu.VMEM((heads, 1), float32),
            pltpu.VMEM((SPAN, width), bfloat16),
            pltpu.VMEM((LANES - 1, rows, width), bfloat16),
            slot_block,
            slot_block,
            slot_block,
            slot_block,
            pltpu.VMEM((LANES - 1, width, units), bfloat16),
            pltpu.VMEM((LANES - 1, width, units), bfloat16),
            pltpu.VMEM((LANES - 1, units, width), bfloat16),
            pltpu.VMEM((width // 128, 128), bfloat16),
            pltpu.VMEM((2, places, width // 128, 128), bfloat16),
            pltpu.VMEM((reqs, width // 128, 128), float32),
            dma((LANES - 1,)),
            dma((LANES - 1,)),
            dma((LANES - 1,)),
            dma((LANES - 1,)),
            dma((4, 3)),
            dma((4, 3)),
            dma((EXPERTS,)),
            dma((EXPERTS,)),
            dma((EXPERTS,)),
            dma((EXPERTS,)),
            dma((LANES - 1,)),
            dma,
            dma((places,)),
            dma((places,)),
            dma((2,)),
            dma((4,)),
        ],
        compiler_params=pltpu.CompilerParams(
            collective_id=0, has_side_effects=True, vmem_limit_bytes=48 * 1024 * 1024
        ),
        name="layer",
    )(
        lengths,
        own_rows,
        cache_keys[0],
        cache_values[0],
        table,
        lane_routes,
        query_weight,
        key_weight,
        value_weight,
        out_weight,
        attention_gain.reshape(1, width),
        expert_gain.reshape(1, width),
        router_weight,
        gate_weight[0],
        up_weight[0],
        down_weight[0],
        final_gain.reshape(1, width),
        order,
        vocab_weight,
    )
    return (layer_rows[None], logits)


def solution(mesh):
    in_specs = (
        P("req", "tp", None),
        P("req", None, "tp"),
        P("req", None, "tp"),
        P(),
        P(),
        P("req", None, None),
        P(None, "tp"),
        P(None, "tp"),
        P(None, "tp"),
        P("tp", None),
        P(),
        P(),
        P(),
        P("req", None, "tp"),
        P("req", None, "tp"),
        P("req", "tp", None),
        P(),
        P(None, ("req", "tp")),
    )
    out_specs = (P("req", "tp", None), P(None, ("req", "tp")))
    return jax.shard_map(body, mesh=mesh, in_specs=in_specs, out_specs=out_specs, check_vma=False)
```

time: 474 us -> 120 us (0.25)
  waiting for transfers between devices: 235 us -> 0 us
  blocking collectives: 135 us -> 0 us
  Pallas kernels: 0 us -> 103 us
  local copies, waits for them, and re-layouts: 38.4 us -> 14 us
  matrix products: 17.4 us -> 0 us
  other arithmetic: 17.1 us -> 0.99 us
  starting transfers between devices: 14.9 us -> 0 us
  between operations: 15 us -> 0.82 us
    all_gather x1 -> x0, waiting for transfers between devices: 121 us -> none  [body(): lax.all_gather(tail_row, ('req', 'tp'), axis=0, tiled=True)]
    all_to_all x1 -> x0, blocking collectives: 115 us -> none  [body(): lax.all_to_all(outgoing, 'req', split_axis=0, concat_axis=0, tiled=True)]
    pallas_call x0 -> x1, Pallas kernels: none -> 103 us  [body(): pl.pallas_call(layer_kernel, out_shape=[jax.ShapeDtypeStruct((rows, width...]
    reduce_scatter x3 -> x0, waiting for transfers between devices: 91.7 us -> none  [the longest x1 47.2 us: body(): lax.psum_scatter(partial_value.astype(jnp.bfloat16), 'tp', scatter_dimens...]
    all_to_all x1 -> x0, waiting for transfers between devices: 21.8 us -> none  [body(): lax.all_to_all(unit_sum, 'req', split_axis=0, concat_axis=0, tiled=True)]
    all_gather x2 -> x0, blocking collectives: 19.9 us -> none  [the longest x1 10.5 us: body(): lax.all_gather(attn_in, 'tp', axis=0, tiled=True)]
    dot_general x11 -> x0, matrix products: 17.4 us -> none  [the longest x1 8.9 us: body(): jnp.einsum('necf,efd->necd', unit_hidden, down_weight, preferred_element_...]
    all_to_all x1 -> x0, starting transfers between devices: 14.5 us -> none  [body(): lax.all_to_all(unit_sum, 'req', split_axis=0, concat_axis=0, tiled=True)]
  transfers between devices with their start and end apart: 5 -> 0, of which waited for: 5 -> 0; matrix products, arithmetic and copies ran while one was open for 3% -> 0% of each run, Pallas kernels for 0% -> 0%
where the time goes in v2:
time: 120 us; the launch traced here: 119 us
  Pallas kernels  103 us (86%)
  local copies, waits for them, and re-layouts  14 us (12%)
    pallas_call x1, Pallas kernels, body(): pl.pallas_call(layer_kernel, out_shape=[jax.ShapeDtypeStruct((rows, width...  103 us
    unnamed x34, local copies, waits for them, and re-layouts  11.5 us

profile of v2, /device:TPU:1, one launch (start us, length us, event | category | flops | bytes accessed | tf_op | source)
XLA Modules:
  0.0 119.0 jit_solution(17212414727333506329)
XLA Ops:
  0.6 0.0 copy-start
  0.6 0.0 copy-start.1
  0.7 1.3 %dynamic_slice.8 = s32[1]{0:T(128)} dynamic-slice(s32[128]{0:T(128)} %length_ref.1, s32[]{:T(128)S(6)} %select_n.6), dynamic_slice_sizes={1} | dynamic-slice | bytes 12 | tf_op jit(solution)/shard_map/dynamic_slice | solution.py:514
  2.0 0.6 add_convert_fusion
  2.7 0.1 mul.44
  2.8 0.0 copy-done
  2.8 0.1 constant_dynamic-slice_fusion
  2.8 0.1 copy.25
  2.9 0.8 reshape.129
  3.7 0.1 copy.26
  3.8 0.1 reshape.130.order_ref
  3.9 0.3 multiply_cosine_fusion
  4.2 1.0 copy.27.router_ref
  5.2 0.0 copy-start.5
  5.2 0.0 copy-start.11
  5.2 0.0 copy-start.12
  5.3 0.0 copy-start.13
  5.3 0.0 copy-start.14
  5.3 1.2 copy.28.vocab_ref
  6.5 0.0 copy-done.1
  6.5 0.0 copy-start.2
  6.5 1.2 %copy-done.2 = bf16[1,4096,128]{2,1,0:T(8,128)(2,1)S(1)} copy-done((bf16[1,4096,128]{2,1,0:T(8,128)(2,1)S(1)}, bf16[1,4096,128]{2,1,0:T(8,128)(2,1)}, u32[]{:S(2)}) %copy-start.2) | copy-done | bytes 1048600
  7.8 1.0 copy-done.3
  8.8 1.0 copy-done.4
  9.9 0.9 copy-done.6
  10.8 0.9 copy-done.7
  11.8 0.9 copy-done.8
  12.7 0.9 copy-done.9
  13.7 0.8 copy-done.10
  14.5 103.2 %layer.1 = (bf16[32,1024]{1,0:T(8,128)(2,1)S(1)}, f32[128,96]{1,0:T(8,128)S(1)}) custom-call(s32[128]{0:T(128)S(1)} %copy-done.14, bf16[32,1024]{1,0:T(8,128)(2,1)S(1)} %bitcast.18, bf16[4096,128]{1,0:T(8,128)(2,1)S(1)} %bitcast.13, bf16[4096,128]{1,0:T(8,128)(2,1)S(1)} %bitcast.14, f32[2,128,128]{2,1,0:T(8,128)S(1)} %pad_maximum_fusion.table_ref, ...), custom_call_target="tpu_custom_call" | custom-call | tf_op jit(solution)/shard_map/layer/pallas_call | solution.py:522
  117.7 0.7 copy.29
  118.4 0.6 copy.31
  (15 shorter events, 0.0 us)
Async XLA Ops:
  0.6 2.1 %copy-start = (s32[1,128,8]{1,2,0:T(8,128)S(1)}, s32[1,128,8]{1,2,0:T(8,128)}, u32[]{:S(2)}) copy-start(s32[1,128,8]{1,2,0:T(8,128)} %param.23) | copy-start | bytes 12292
  0.6 5.8 %copy-start.1 = (bf16[1,4096,128]{2,1,0:T(8,128)(2,1)S(1)}, bf16[1,4096,128]{2,1,0:T(8,128)(2,1)}, u32[]{:S(2)}) copy-start(bf16[1,4096,128]{2,1,0:T(8,128)(2,1)} %param.19) | copy-start | bytes 3145732
  5.2 1.3 %copy-start.5 = (bf16[1024,128]{1,0:T(8,128)(2,1)S(1)}, bf16[1024,128]{1,0:T(8,128)(2,1)}, u32[]{:S(2)}) copy-start(bf16[1024,128]{1,0:T(8,128)(2,1)} %key_ref.1) | copy-start | bytes 786436
  5.2 1.3 %copy-start.11 = (f32[1024]{0:T(1024)S(1)}, f32[1024]{0:T(1024)}, u32[]{:S(2)}) copy-start(f32[1024]{0:T(1024)} %param.28) | copy-start | bytes 12292
  5.2 1.3 %copy-start.12 = (f32[1024]{0:T(1024)S(1)}, f32[1024]{0:T(1024)}, u32[]{:S(2)}) copy-start(f32[1024]{0:T(1024)} %param.29) | copy-start | bytes 12292
  5.3 1.3 %copy-start.13 = (f32[1024]{0:T(1024)S(1)}, f32[1024]{0:T(1024)}, u32[]{:S(2)}) copy-start(f32[1024]{0:T(1024)} %param.34) | copy-start | bytes 12292
  5.3 1.3 %copy-start.14 = (s32[128]{0:T(128)S(1)}, s32[128]{0:T(128)}, u32[]{:S(2)}) copy-start(s32[128]{0:T(128)} %length_ref.1) | copy-start | bytes 1540
  6.5 1.2 %copy-start.2 = (bf16[1,4096,128]{2,1,0:T(8,128)(2,1)S(1)}, bf16[1,4096,128]{2,1,0:T(8,128)(2,1)}, u32[]{:S(2)}) copy-start(bf16[1,4096,128]{2,1,0:T(8,128)(2,1)} %param.20) | copy-start | bytes 3145732
  7.8 1.0 copy-start.3
  8.8 1.0 copy-start.4
  9.9 0.9 copy-start.6
  10.8 0.9 copy-start.7
  11.8 0.9 copy-start.8
  12.7 0.9 copy-start.9
  13.7 0.8 copy-start.10

commit v3 on v2

--- a/solution.py
+++ b/solution.py
@@ -1,5 +1,6 @@
 import jax
 import jax.numpy as jnp
+import numpy as np
 from jax.experimental import pallas as pl
 from jax.experimental.pallas import tpu as pltpu
 from jax import lax
@@ -73,11 +74,31 @@
 
 
 def layer_kernel(
+    frequency_ref,
+    length_hbm,
+    own_hbm,
+    keys_hbm,
+    values_hbm,
+    routes_hbm,
+    query_hbm,
+    key_hbm,
+    value_hbm,
+    out_hbm,
+    attention_gain_hbm,
+    expert_gain_hbm,
+    router_hbm,
+    gate_hbm,
+    up_hbm,
+    down_hbm,
+    final_gain_hbm,
+    order_hbm,
+    vocab_hbm,
+    layer_ref,
+    logits_ref,
     length_ref,
     own_ref,
     keys_ref,
     values_ref,
-    table_ref,
     routes_ref,
     query_ref,
     key_ref,
@@ -92,8 +113,6 @@
     final_gain_ref,
     order_ref,
     vocab_ref,
-    layer_ref,
-    logits_ref,
     normed,
     all_rows,
     stacked,
@@ -127,6 +146,7 @@
     plane_recv,
     core_sem,
     local_sem,
+    load_sem,
 ):
     req, me = lax.axis_index("req"), lax.axis_index("tp")
     z, y, core = req // (2 * RING_Y), lax.rem(req // 2, RING_Y), lax.rem(req, 2)
@@ -153,10 +173,45 @@
     def _(step):
         greet(barrier, plane_peer(step))
 
+    loads = {}
+    for number, (name, source, held) in enumerate(
+        (
+            ("own", own_hbm, own_ref),
+            ("attention_gain", attention_gain_hbm, attention_gain_ref),
+            ("length", length_hbm, length_ref),
+            ("keys", keys_hbm, keys_ref),
+            ("values", values_hbm, values_ref),
+            ("routes", routes_hbm, routes_ref),
+            ("query", query_hbm, query_ref),
+            ("key", key_hbm, key_ref),
+            ("value", value_hbm, value_ref),
+            ("out", out_hbm, out_ref),
+            ("expert_gain", expert_gain_hbm, expert_gain_ref),
+            ("router", router_hbm, router_ref),
+            ("gate", gate_hbm, gate_ref),
+            ("up", up_hbm, up_ref),
+            ("down", down_hbm, down_ref),
+            ("final_gain", final_gain_hbm, final_gain_ref),
+            ("order", order_hbm, order_ref),
+            ("vocab", vocab_hbm, vocab_ref),
+        )
+    ):
+        loads[name] = pltpu.make_async_copy(source, held, load_sem.at[number])
+        loads[name].start()
+
+    def ready(*wanted):
+        for name in wanted:
+            loads[name].wait()
+
+    ready("own", "attention_gain", "length")
     normed[...] = rms_scale(own_ref[...], attention_gain_ref[...]).astype(bfloat16)
     own_place = pl.ds(pl.multiple_of(me * rows, rows), rows)
     local = pltpu.make_async_copy(normed, all_rows.at[own_place], local_sem.at[0])
     local.start()
+    length = length_ref[req]
+    positions = (length + iota((SPAN, 128), 0)).astype(float32)
+    angles = positions * frequency_ref[...]
+    cosine, sine = jnp.cos(angles), jnp.sin(angles)
     pl.semaphore_wait(barrier, LANES - 1 + 1 + places - 1)
 
     row_copies = [
@@ -165,7 +220,7 @@
     ]
     for copy in row_copies:
         copy.start()
-    triples = ((gate_ref, gates), (up_ref, ups), (down_ref, downs))
+    triples = ((gate_hbm, gates), (up_hbm, ups), (down_hbm, downs))
 
     def near_weights():
         return [
@@ -206,7 +261,6 @@
     lanes_at = iota((SPAN, 128), 1)
     front = lax.rem(lanes_at, HEAD_DIM) < HEAD_DIM // 2
     first_head = lanes_at < HEAD_DIM
-    cosine, sine = table_ref[0], table_ref[1]
     token_rows = all_rows[...]
 
     def turned(piece):
@@ -215,6 +269,7 @@
         )
         return piece * cosine + other * sine
 
+    ready("query", "key", "value")
     projected = dot(token_rows, query_ref[...])
     zero = jnp.zeros((SPAN, 128), float32)
     for group in range(2):
@@ -233,7 +288,7 @@
     expo = jnp.where(causal, jnp.exp(dot_last(stacked[...], new_keys)), 0.0)
     numerator[...] = dot(expo.astype(bfloat16), new_values)
     denominator[...] = jnp.sum(expo, axis=-1, keepdims=True)
-    length = length_ref[req]
+    ready("keys", "values")
 
     @pl.loop(0, keys_ref.shape[0] // key_block)
     def _(number):
@@ -244,6 +299,7 @@
         numerator[...] += dot(block.astype(bfloat16), values_ref[at, :])
         denominator[...] += jnp.sum(block, axis=-1, keepdims=True)
 
+    ready("out")
     mean_values = numerator[...] / denominator[...]
     head = [mean_values[at * SPAN : (at + 1) * SPAN] for at in range(4)]
     attended = jnp.concatenate(
@@ -277,14 +333,17 @@
     for step, copy in enumerate(mix_copies):
         copy.wait()
         total = total + part_held[step].astype(float32)
+    ready("expert_gain", "router", "routes")
     mixed = (own_ref[...].astype(float32) + total).astype(bfloat16)
     expert_in = rms_scale(mixed, expert_gain_ref[...]).astype(bfloat16)
 
-    expert_at = iota((rows, EXPERTS), 1)
-    named = jnp.zeros((rows, EXPERTS), float32)
+    expert_at = iota((EXPERTS, SPAN), 0)
+    every_named = jnp.zeros((EXPERTS, SPAN), float32)
     for choice in range(TOPK):
-        named = named + jnp.where(routes_ref[:, choice : choice + 1] == expert_at, 1.0, 0.0)
-    gate_expo = jnp.where(named > 0.0, jnp.exp(dot(expert_in, router_ref[...])), 0.0)
+        every_named = every_named + jnp.where(routes_ref[choice : choice + 1, :] == expert_at, 1.0, 0.0)
+    own_tokens = one_hot(iota((rows, SPAN), 1) == iota((rows, SPAN), 0) + me * rows)
+    named = dot_last(own_tokens, every_named.astype(bfloat16))
+    gate_expo = jnp.where(named > 0.0, jnp.exp(dot_last(expert_in, router_ref[...])), 0.0)
     gate_values = (gate_expo / jnp.sum(gate_expo, axis=-1, keepdims=True)).astype(bfloat16)
     earlier = one_hot(iota((rows, rows), 1) < iota((rows, rows), 0))
     ranks = jnp.where(named > 0.0, dot(earlier, named.astype(bfloat16)), 99.0).astype(bfloat16)
@@ -343,6 +402,7 @@
     for copy in far_weights():
         copy.wait()
 
+    ready("gate", "up", "down")
     group = 8
     group_rows = group * SLOT_ROWS
     row_at, column_at = iota((group_rows, group_rows), 0), iota((group_rows, group_rows), 1)
@@ -465,6 +525,7 @@
     half.start()
     half.wait()
 
+    ready("final_gain", "order", "vocab")
     count = 2 * places
     tails_wide[...] = tails[...].astype(float32).reshape(count, parts, 128)
     square = jnp.zeros((count, 1), float32)
@@ -472,13 +533,16 @@
         piece = tails_wide[:, at, :]
         square = square + jnp.sum(piece * piece, axis=-1, keepdims=True)
     scale = lax.rsqrt(square / width + epsilon)
-    chosen = one_hot(iota((count, count), 0) == order_ref[...])
+    by_slot = one_hot(iota((count, count), 0) == order_ref[...])
+    slot_at, held_at = iota((count, count), 0), iota((count, count), 1)
+    held_slot = lax.rem(held_at, places) * 2 + held_at // places
+    chosen = dot(by_slot, one_hot(slot_at == held_slot)).astype(bfloat16)
     found = jnp.zeros(logits_ref.shape, float32)
     for at in range(parts):
         span = slice(at * 128, (at + 1) * 128)
         final = (tails_wide[:, at, :] * scale * final_gain_ref[:, span]).astype(bfloat16)
         ordered = dot(chosen, final).astype(bfloat16)
-        found = found + dot(ordered, vocab_ref[span, :])
+        found = found + dot_last(vocab_ref[:, span], ordered)
     logits_ref[...] = found
 
 
@@ -508,14 +572,28 @@
     reqs = lengths.shape[0]
     places = reqs // 2
     half_dim = HEAD_DIM // 2
-    frequency = jnp.exp(
-        -jnp.log(10000.0) * jnp.arange(half_dim, dtype=float32) * (2.0 / HEAD_DIM)
-    )
-    positions = lengths[lax.axis_index("req")] + jnp.arange(SPAN, dtype=jnp.int32)
-    angles = positions.astype(float32)[:, None] * jnp.tile(frequency, 128 // half_dim)[None, :]
-    table = jnp.stack([jnp.cos(angles), jnp.sin(angles)])
-    lane_routes = lax.dynamic_slice_in_dim(routes[0], lax.axis_index("tp") * rows, rows, 0)
-    order = request_order.reshape(places, 2).T.reshape(1, reqs)
+    frequency = np.exp(-np.log(10000.0) * np.arange(half_dim) * (2.0 / HEAD_DIM)).astype(np.float32)
+    frequency = jnp.asarray(np.tile(frequency, 128 // half_dim)[None, :])
+    operands = [
+        lengths,
+        own_rows,
+        cache_keys[0],
+        cache_values[0],
+        routes[0].T,
+        query_weight,
+        key_weight,
+        value_weight,
+        out_weight,
+        attention_gain.reshape(1, width),
+        expert_gain.reshape(1, width),
+        router_weight.T,
+        gate_weight[0],
+        up_weight[0],
+        down_weight[0],
+        final_gain.reshape(1, width),
+        request_order.reshape(1, reqs),
+        vocab_weight.T,
+    ]
     dma = pltpu.SemaphoreType.DMA
     heads = 4 * SPAN
     slot_block = pltpu.VMEM((EXPERTS, SLOT_ROWS, PACKED), bfloat16)
@@ -523,11 +601,13 @@
         layer_kernel,
         out_shape=[
             jax.ShapeDtypeStruct((rows, width), bfloat16),
-            jax.ShapeDtypeStruct((reqs, vocab_weight.shape[1]), float32),
+            jax.ShapeDtypeStruct((vocab_weight.shape[1], reqs), float32),
         ],
-        in_specs=[pl.BlockSpec(memory_space=pltpu.SMEM)] + [VMEM_SPEC] * 18,
+        in_specs=[VMEM_SPEC] + [pl.BlockSpec(memory_space=pltpu.HBM)] * len(operands),
         out_specs=[VMEM_SPEC] * 2,
-        scratch_shapes=[
+        scratch_shapes=[pltpu.SMEM((reqs,), jnp.int32)]
+        + [pltpu.VMEM(operand.shape, operand.dtype) for operand in operands[1:]]
+        + [
             pltpu.VMEM((rows, width), bfloat16),
             pltpu.VMEM((SPAN, width), bfloat16),
             pltpu.VMEM((heads, 128), bfloat16),
@@ -561,33 +641,14 @@
             dma((places,)),
             dma((2,)),
             dma((4,)),
+            dma((len(operands),)),
         ],
         compiler_params=pltpu.CompilerParams(
-            collective_id=0, has_side_effects=True, vmem_limit_bytes=48 * 1024 * 1024
+            collective_id=0, has_side_effects=True, vmem_limit_bytes=67043328
         ),
         name="layer",
-    )(
-        lengths,
-        own_rows,
-        cache_keys[0],
-        cache_values[0],
-        table,
-        lane_routes,
-        query_weight,
-        key_weight,
-        value_weight,
-        out_weight,
-        attention_gain.reshape(1, width),
-        expert_gain.reshape(1, width),
-        router_weight,
-        gate_weight[0],
-        up_weight[0],
-        down_weight[0],
-        final_gain.reshape(1, width),
-        order,
-        vocab_weight,
-    )
-    return (layer_rows[None], logits)
+    )(frequency, *operands)
+    return (layer_rows[None], logits.T)
 
 
 def solution(mesh):

time: 120 us -> 106 us (0.88)
  local copies, waits for them, and re-layouts: 14 us -> 2.11 us
    unnamed x34 -> x4, local copies, waits for them, and re-layouts: 11.5 us -> 2.11 us
    dynamic_slice x3 -> x0, local copies, waits for them, and re-layouts: 1.48 us -> none  [the longest x1 1.33 us: body(): lengths[lax.axis_index('req')] + jnp.arange(SPAN, dtype=jnp.int32)]
where the time goes in v3:
time: 106 us
  Pallas kernels  103 us (97%)
  local copies, waits for them, and re-layouts  2.11 us (2%)
    pallas_call x1, Pallas kernels, body(): pl.pallas_call(layer_kernel, out_shape=[jax.ShapeDtypeStruct((rows, width...  103 us

profile of v3, /device:TPU:1, one launch (start us, length us, event | category | flops | bytes accessed | tf_op | source)
XLA Modules:
  0.0 105.9 jit_solution(8186467643137161251)
XLA Ops:
  0.6 103.1 %layer.1 = (bf16[32,1024]{1,0:T(8,128)(2,1)}, f32[96,128]{1,0:T(8,128)}) custom-call(f32[1,128]{1,0:T(1,128)} %constant.2.clone.frequency_ref, s32[128]{0:T(128)} %length_hbm.1, bf16[32,1024]{1,0:T(8,128)(2,1)} %bitcast.23, bf16[4096,128]{1,0:T(8,128)(2,1)} %bitcast.17, bf16[4096,128]{1,0:T(8,128)(2,1)} %bitcast.18, s32[8,128]{1,0:T(8,128)} %bitcast.27, ...), custom_call_target="tpu_custom_call" | custom-call | tf_op jit(solution)/shard_map/layer/pallas_call | solution.py:600
  103.8 0.0 copy-start
  103.8 1.5 %copy.23 = bf16[1,32,1024]{2,1,0:T(8,128)(2,1)} copy(bf16[1,32,1024]{2,1,0:T(8,128)(2,1)} %bitcast.25) | data formatting | bytes 131072
  105.3 0.0 copy-done
  105.3 0.6 copy.24
Async XLA Ops:
  103.8 1.5 %copy-start = (f32[96,128]{1,0:T(8,128)S(1)}, f32[96,128]{1,0:T(8,128)}, u32[]{:S(2)}) copy-start(f32[96,128]{1,0:T(8,128)} %get-tuple-element.5) | copy-start | bytes 147460

commit v4 on v3

--- a/solution.py
+++ b/solution.py
@@ -107,9 +107,6 @@
     attention_gain_ref,
     expert_gain_ref,
     router_ref,
-    gate_ref,
-    up_ref,
-    down_ref,
     final_gain_ref,
     order_ref,
     vocab_ref,
@@ -124,9 +121,8 @@
     arrived,
     result,
     back,
-    gates,
-    ups,
-    downs,
+    entry,
+    exit_rows,
     tail,
     tails,
     tails_wide,
@@ -155,6 +151,8 @@
     mine = place // 2
     experts, _, _ = outgoing.shape
     rows, width = own_ref.shape
+    units = down_hbm.shape[0]
+    pair = 2 * units
     partner = z * 2 * RING_Y + y * 2 + 1 - core
     last = LANES - 1
     barrier = pltpu.get_barrier_semaphore()
@@ -188,9 +186,9 @@
             ("out", out_hbm, out_ref),
             ("expert_gain", expert_gain_hbm, expert_gain_ref),
             ("router", router_hbm, router_ref),
-            ("gate", gate_hbm, gate_ref),
-            ("up", up_hbm, up_ref),
-            ("down", down_hbm, down_ref),
+            ("gate", gate_hbm, entry.at[:, :units]),
+            ("up", up_hbm, entry.at[:, units : 2 * units]),
+            ("down", down_hbm, exit_rows.at[:units]),
             ("final_gain", final_gain_hbm, final_gain_ref),
             ("order", order_hbm, order_ref),
             ("vocab", vocab_hbm, vocab_ref),
@@ -220,36 +218,61 @@
     ]
     for copy in row_copies:
         copy.start()
-    triples = ((gate_hbm, gates), (up_hbm, ups), (down_hbm, downs))
+    half = width // 2
+    own_half = pl.ds(pl.multiple_of(core * half, half), half)
+
+    def exit_at(slot, amount, side):
+        first = slot * units + core * (units // 2) + side * amount
+        return pl.ds(pl.multiple_of(first, amount), amount)
+
+    def weight_copy(source, target, number, device):
+        return send(source, target, weight_send.at[number], weight_recv.at[number], device)
 
     def near_weights():
-        return [
-            send(
-                source,
-                target.at[side],
-                weight_send.at[side, number],
-                weight_recv.at[side, number],
-                lane((1, LANES - 1)[side]),
-            )
-            for number, (source, target) in enumerate(triples)
-            for side in range(2)
-        ]
+        found = []
+        for side in range(2):
+            first = (1 + side) * pair
+            to = lane((1, LANES - 1)[side])
+            unit_half = pl.ds(pl.multiple_of(core * (units // 2), units // 2), units // 2)
+            for number, (source, target) in enumerate(
+                (
+                    (gate_hbm.at[own_half], entry.at[own_half, first : first + units]),
+                    (up_hbm.at[own_half], entry.at[own_half, first + units : first + pair]),
+                    (down_hbm.at[unit_half], exit_rows.at[exit_at(1 + side, units // 2, 0)]),
+                )
+            ):
+                found.append(weight_copy(source, target, side * 3 + number, to))
+        return found
 
     def far_weights():
         found = []
-        for number, (source, target) in enumerate(triples):
-            half = source.shape[0] // 2
-            for side in range(2):
-                piece = pl.ds(side * half, half)
-                found.append(
-                    send(
-                        target.at[side, piece],
-                        target.at[2, piece],
-                        weight_send.at[2 + side, number],
-                        weight_recv.at[2 + side, number],
-                        lane((1, LANES - 1)[side]),
-                    )
+        quarter = half // 2
+        for side in range(2):
+            first = (1 + side) * pair
+            to = lane((1, LANES - 1)[side])
+            at = pl.ds(pl.multiple_of(core * half + side * quarter, quarter), quarter)
+            found.append(
+                weight_copy(
+                    entry.at[at, first : first + pair], entry.at[at, 3 * pair :], 6 + side * 2, to
                 )
+            )
+            found.append(
+                weight_copy(
+                    exit_rows.at[exit_at(1 + side, units // 4, side)],
+                    exit_rows.at[exit_at(3, units // 4, side)],
+                    7 + side * 2,
+                    to,
+                )
+            )
+        return found
+
+    def chip_weights(far):
+        columns = slice(3 * pair, 4 * pair) if far else slice(pair, 3 * pair)
+        place_in = entry.at[own_half, columns]
+        found = [weight_copy(place_in, place_in, 10 + far, (partner, me))]
+        for slot in (3,) if far else (1, 2):
+            block = exit_rows.at[exit_at(slot, units // 2, 0)]
+            found.append(weight_copy(block, block, 11 + slot, (partner, me)))
         return found
 
     for copy in near_weights():
@@ -277,10 +300,10 @@
         piece = piece * HEAD_DIM ** (-0.5)
         swapped = pltpu.roll(piece, HEAD_DIM, 1)
         keep = first_head if group == 0 else jnp.logical_not(first_head)
-        pair = (piece, swapped) if group == 0 else (swapped, piece)
+        members = (piece, swapped) if group == 0 else (swapped, piece)
         for member in range(2):
             at = (group * 2 + member) * SPAN
-            stacked[at : at + SPAN, :] = jnp.where(keep, pair[member], zero).astype(bfloat16)
+            stacked[at : at + SPAN, :] = jnp.where(keep, members[member], zero).astype(bfloat16)
     new_keys = turned(dot(token_rows, key_ref[...])).astype(bfloat16)
     new_values = dot(token_rows, value_ref[...]).astype(bfloat16)
     heads = 4 * SPAN
@@ -327,7 +350,7 @@
         copy.start()
     for copy in near_weights():
         copy.wait()
-    for copy in far_weights():
+    for copy in far_weights() + chip_weights(False):
         copy.start()
     total = part[own_place, :].astype(float32)
     for step, copy in enumerate(mix_copies):
@@ -401,6 +424,10 @@
     own_block.wait()
     for copy in far_weights():
         copy.wait()
+    for copy in chip_weights(True):
+        copy.start()
+    for copy in chip_weights(False) + chip_weights(True):
+        copy.wait()
 
     ready("gate", "up", "down")
     group = 8
@@ -428,16 +455,13 @@
             moved = dot(unpacks[chunk], block[:, chunk * CHUNK : (chunk + 1) * CHUNK])
             end = moved if end is None else end + moved
         whole = jnp.concatenate([block, end.astype(bfloat16)], axis=1)
-        total = None
+        entered = dot(whole, entry[...])
+        hidden = []
         for held in range(LANES):
-            gate_block = gate_ref[...] if held == 0 else gates[held - 1]
-            up_block = up_ref[...] if held == 0 else ups[held - 1]
-            down_block = down_ref[...] if held == 0 else downs[held - 1]
-            gate_part = dot(whole, gate_block)
-            up_part = dot(whole, up_block)
-            hidden = (gate_part / (1.0 + jnp.exp(-gate_part)) * up_part).astype(bfloat16)
-            term = dot(hidden, down_block)
-            total = term if total is None else total + term
+            gate_part = entered[:, held * pair : held * pair + units]
+            up_part = entered[:, held * pair + units : (held + 1) * pair]
+            hidden.append((gate_part / (1.0 + jnp.exp(-gate_part)) * up_part).astype(bfloat16))
+        total = dot(jnp.concatenate(hidden, axis=1), exit_rows[...])
         rounded = total.astype(bfloat16)
         for chunk in range(chunks):
             span = slice(chunk * CHUNK, (chunk + 1) * CHUNK)
@@ -521,9 +545,9 @@
     def _(step):
         plane_copy(step).wait()
 
-    half = send(tails.at[core], tails.at[core], core_sem.at[0], core_sem.at[1], (partner, me))
-    half.start()
-    half.wait()
+    other_half = send(tails.at[core], tails.at[core], core_sem.at[0], core_sem.at[1], (partner, me))
+    other_half.start()
+    other_half.wait()
 
     ready("final_gain", "order", "vocab")
     count = 2 * places
@@ -606,7 +630,7 @@
         in_specs=[VMEM_SPEC] + [pl.BlockSpec(memory_space=pltpu.HBM)] * len(operands),
         out_specs=[VMEM_SPEC] * 2,
         scratch_shapes=[pltpu.SMEM((reqs,), jnp.int32)]
-        + [pltpu.VMEM(operand.shape, operand.dtype) for operand in operands[1:]]
+        + [pltpu.VMEM(operand.shape, operand.dtype) for operand in operands[1:12] + operands[15:]]
         + [
             pltpu.VMEM((rows, width), bfloat16),
             pltpu.VMEM((SPAN, width), bfloat16),
@@ -619,9 +643,8 @@
             slot_block,
             slot_block,
             slot_block,
-            pltpu.VMEM((LANES - 1, width, units), bfloat16),
-            pltpu.VMEM((LANES - 1, width, units), bfloat16),
-            pltpu.VMEM((LANES - 1, units, width), bfloat16),
+            pltpu.VMEM((width, LANES * 2 * units), bfloat16),
+            pltpu.VMEM((LANES * units, width), bfloat16),
             pltpu.VMEM((width // 128, 128), bfloat16),
             pltpu.VMEM((2, places, width // 128, 128), bfloat16),
             pltpu.VMEM((reqs, width // 128, 128), float32),
@@ -629,8 +652,8 @@
             dma((LANES - 1,)),
             dma((LANES - 1,)),
             dma((LANES - 1,)),
-            dma((4, 3)),
-            dma((4, 3)),
+            dma((15,)),
+            dma((15,)),
             dma((EXPERTS,)),
             dma((EXPERTS,)),
             dma((EXPERTS,)),

time: 106 us -> 99.5 us (0.939)
  Pallas kernels: 103 us -> 96.5 us
    pallas_call x1, Pallas kernels: 103 us -> 96.5 us  [body(): pl.pallas_call(layer_kernel, out_shape=[jax.ShapeDtypeStruct((rows, width...]
where the time goes in v4:
time: 99.5 us; the launch traced here: 99.3 us
  Pallas kernels  96.5 us (97%)
  local copies, waits for them, and re-layouts  2.11 us (2%)
    pallas_call x1, Pallas kernels, body(): pl.pallas_call(layer_kernel, out_shape=[jax.ShapeDtypeStruct((rows, width...  96.5 us
    unnamed x4, local copies, waits for them, and re-layouts  2.11 us

profile of v4, /device:TPU:1, one launch (start us, length us, event | category | flops | bytes accessed | tf_op | source)
XLA Modules:
  0.0 99.3 jit_solution(5528290946926093113)
XLA Ops:
  0.6 96.5 %layer.1 = (bf16[32,1024]{1,0:T(8,128)(2,1)}, f32[96,128]{1,0:T(8,128)}) custom-call(f32[1,128]{1,0:T(1,128)} %constant.2.clone.frequency_ref, s32[128]{0:T(128)} %length_hbm.1, bf16[32,1024]{1,0:T(8,128)(2,1)} %bitcast.23, bf16[4096,128]{1,0:T(8,128)(2,1)} %bitcast.17, bf16[4096,128]{1,0:T(8,128)(2,1)} %bitcast.18, s32[8,128]{1,0:T(8,128)} %bitcast.27, ...), custom_call_target="tpu_custom_call" | custom-call | tf_op jit(solution)/shard_map/layer/pallas_call | solution.py:624
  97.2 0.0 copy-start
  97.2 1.5 %copy.23 = bf16[1,32,1024]{2,1,0:T(8,128)(2,1)} copy(bf16[1,32,1024]{2,1,0:T(8,128)(2,1)} %bitcast.25) | data formatting | bytes 131072
  98.7 0.0 copy-done
  98.7 0.6 copy.24
Async XLA Ops:
  97.2 1.5 %copy-start = (f32[96,128]{1,0:T(8,128)S(1)}, f32[96,128]{1,0:T(8,128)}, u32[]{:S(2)}) copy-start(f32[96,128]{1,0:T(8,128)} %get-tuple-element.5) | copy-start | bytes 147460

commit v5 on v4

--- a/solution.py
+++ b/solution.py
@@ -210,6 +210,40 @@
     positions = (length + iota((SPAN, 128), 0)).astype(float32)
     angles = positions * frequency_ref[...]
     cosine, sine = jnp.cos(angles), jnp.sin(angles)
+    ready("routes", "order")
+    expert_at = iota((EXPERTS, SPAN), 0)
+    every_named = jnp.zeros((EXPERTS, SPAN), float32)
+    for choice in range(TOPK):
+        every_named = every_named + jnp.where(routes_ref[choice : choice + 1, :] == expert_at, 1.0, 0.0)
+    own_tokens = one_hot(iota((rows, SPAN), 1) == iota((rows, SPAN), 0) + me * rows)
+    named = dot_last(own_tokens, every_named.astype(bfloat16))
+    earlier = one_hot(iota((rows, rows), 1) < iota((rows, rows), 0))
+    ranks = jnp.where(named > 0.0, dot(earlier, named.astype(bfloat16)), 99.0).astype(bfloat16)
+    slots = EXPERTS * SLOT_ROWS
+    spread = one_hot(iota((slots, EXPERTS), 0) // SLOT_ROWS == iota((slots, EXPERTS), 1))
+    slot_rank = dot_last(spread, ranks)
+    slot_row = lax.rem(iota((slots, rows), 0), SLOT_ROWS)
+    chunks = PACKED // CHUNK
+
+    def picker(chunk):
+        return one_hot(slot_rank == packed_rank(slot_row, chunk).astype(float32))
+
+    main_picker = picker(None)
+    end_pickers = [picker(chunk) for chunk in range(chunks)]
+    group = 8
+    group_rows = group * SLOT_ROWS
+    row_at, column_at = iota((group_rows, group_rows), 0), iota((group_rows, group_rows), 1)
+    same_slot = row_at // SLOT_ROWS == column_at // SLOT_ROWS
+    row_in, column_in = lax.rem(row_at, SLOT_ROWS), lax.rem(column_at, SLOT_ROWS)
+    kept = one_hot(same_slot & (packed_rank(row_in, None) == column_in))
+    packs = [one_hot(same_slot & (packed_rank(row_in, chunk) == column_in)) for chunk in range(chunks)]
+    unpacks = [one_hot(same_slot & (packed_rank(column_in, chunk) == row_in)) for chunk in range(chunks)]
+
+    count = 2 * places
+    by_slot = one_hot(iota((count, count), 0) == order_ref[...])
+    slot_at, held_at = iota((count, count), 0), iota((count, count), 1)
+    held_slot = lax.rem(held_at, places) * 2 + held_at // places
+    chosen = dot(by_slot, one_hot(slot_at == held_slot)).astype(bfloat16)
     pl.semaphore_wait(barrier, LANES - 1 + 1 + places - 1)
 
     row_copies = [
@@ -295,14 +329,14 @@
     ready("query", "key", "value")
     projected = dot(token_rows, query_ref[...])
     zero = jnp.zeros((SPAN, 128), float32)
-    for group in range(2):
-        piece = turned(projected[:, group * 128 : (group + 1) * 128]).astype(bfloat16).astype(float32)
+    for block_at in range(2):
+        piece = turned(projected[:, block_at * 128 : (block_at + 1) * 128]).astype(bfloat16).astype(float32)
         piece = piece * HEAD_DIM ** (-0.5)
         swapped = pltpu.roll(piece, HEAD_DIM, 1)
-        keep = first_head if group == 0 else jnp.logical_not(first_head)
-        members = (piece, swapped) if group == 0 else (swapped, piece)
+        keep = first_head if block_at == 0 else jnp.logical_not(first_head)
+        members = (piece, swapped) if block_at == 0 else (swapped, piece)
         for member in range(2):
-            at = (group * 2 + member) * SPAN
+            at = (block_at * 2 + member) * SPAN
             stacked[at : at + SPAN, :] = jnp.where(keep, members[member], zero).astype(bfloat16)
     new_keys = turned(dot(token_rows, key_ref[...])).astype(bfloat16)
     new_values = dot(token_rows, value_ref[...]).astype(bfloat16)
@@ -356,33 +390,15 @@
     for step, copy in enumerate(mix_copies):
         copy.wait()
         total = total + part_held[step].astype(float32)
-    ready("expert_gain", "router", "routes")
+    ready("expert_gain", "router")
     mixed = (own_ref[...].astype(float32) + total).astype(bfloat16)
     expert_in = rms_scale(mixed, expert_gain_ref[...]).astype(bfloat16)
 
-    expert_at = iota((EXPERTS, SPAN), 0)
-    every_named = jnp.zeros((EXPERTS, SPAN), float32)
-    for choice in range(TOPK):
-        every_named = every_named + jnp.where(routes_ref[choice : choice + 1, :] == expert_at, 1.0, 0.0)
-    own_tokens = one_hot(iota((rows, SPAN), 1) == iota((rows, SPAN), 0) + me * rows)
-    named = dot_last(own_tokens, every_named.astype(bfloat16))
     gate_expo = jnp.where(named > 0.0, jnp.exp(dot_last(expert_in, router_ref[...])), 0.0)
     gate_values = (gate_expo / jnp.sum(gate_expo, axis=-1, keepdims=True)).astype(bfloat16)
-    earlier = one_hot(iota((rows, rows), 1) < iota((rows, rows), 0))
-    ranks = jnp.where(named > 0.0, dot(earlier, named.astype(bfloat16)), 99.0).astype(bfloat16)
-    slots = EXPERTS * SLOT_ROWS
-    spread = one_hot(iota((slots, EXPERTS), 0) // SLOT_ROWS == iota((slots, EXPERTS), 1))
-    slot_rank = dot_last(spread, ranks)
-    slot_row = lax.rem(iota((slots, rows), 0), SLOT_ROWS)
-    chunks = PACKED // CHUNK
-
-    def picker(chunk):
-        return one_hot(slot_rank == packed_rank(slot_row, chunk).astype(float32))
-
-    main = picker(None)
     for chunk in range(chunks):
         span = slice(chunk * CHUNK, (chunk + 1) * CHUNK)
-        piece = dot(main, expert_in[:, span]) + dot(picker(chunk), expert_in[:, PACKED:])
+        piece = dot(main_picker, expert_in[:, span]) + dot(end_pickers[chunk], expert_in[:, PACKED:])
         outgoing[:, :, span] = piece.astype(bfloat16).reshape(EXPERTS, SLOT_ROWS, CHUNK)
 
     def target(step):
@@ -430,15 +446,6 @@
         copy.wait()
 
     ready("gate", "up", "down")
-    group = 8
-    group_rows = group * SLOT_ROWS
-    row_at, column_at = iota((group_rows, group_rows), 0), iota((group_rows, group_rows), 1)
-    same_slot = row_at // SLOT_ROWS == column_at // SLOT_ROWS
-    row_in, column_in = lax.rem(row_at, SLOT_ROWS), lax.rem(column_at, SLOT_ROWS)
-    kept = one_hot(same_slot & (packed_rank(row_in, None) == column_in))
-    packs = [one_hot(same_slot & (packed_rank(row_in, chunk) == column_in)) for chunk in range(chunks)]
-    unpacks = [one_hot(same_slot & (packed_rank(column_in, chunk) == row_in)) for chunk in range(chunks)]
-
     @pl.loop(0, experts // group)
     def _(number):
         first = number * group
@@ -549,18 +556,13 @@
     other_half.start()
     other_half.wait()
 
-    ready("final_gain", "order", "vocab")
-    count = 2 * places
+    ready("final_gain", "vocab")
     tails_wide[...] = tails[...].astype(float32).reshape(count, parts, 128)
     square = jnp.zeros((count, 1), float32)
     for at in range(parts):
         piece = tails_wide[:, at, :]
         square = square + jnp.sum(piece * piece, axis=-1, keepdims=True)
     scale = lax.rsqrt(square / width + epsilon)
-    by_slot = one_hot(iota((count, count), 0) == order_ref[...])
-    slot_at, held_at = iota((count, count), 0), iota((count, count), 1)
-    held_slot = lax.rem(held_at, places) * 2 + held_at // places
-    chosen = dot(by_slot, one_hot(slot_at == held_slot)).astype(bfloat16)
     found = jnp.zeros(logits_ref.shape, float32)
     for at in range(parts):
         span = slice(at * 128, (at + 1) * 128)

time: 99.5 us -> 95.9 us (0.964)
  Pallas kernels: 96.5 us -> 93 us
    pallas_call x1, Pallas kernels: 96.5 us -> 93 us  [body(): pl.pallas_call(layer_kernel, out_shape=[jax.ShapeDtypeStruct((rows, width...]
where the time goes in v5:
time: 95.9 us; the launch traced here: 95.7 us
  Pallas kernels  93 us (97%)
  local copies, waits for them, and re-layouts  2.11 us (2%)
    pallas_call x1, Pallas kernels, body(): pl.pallas_call(layer_kernel, out_shape=[jax.ShapeDtypeStruct((rows, width...  93 us
    unnamed x4, local copies, waits for them, and re-layouts  2.11 us

profile of v5, /device:TPU:1, one launch (start us, length us, event | category | flops | bytes accessed | tf_op | source)
XLA Modules:
  0.0 95.7 jit_solution(229552560069792762)
XLA Ops:
  0.6 93.0 %layer.1 = (bf16[32,1024]{1,0:T(8,128)(2,1)}, f32[96,128]{1,0:T(8,128)}) custom-call(f32[1,128]{1,0:T(1,128)} %constant.2.clone.frequency_ref, s32[128]{0:T(128)} %length_hbm.1, bf16[32,1024]{1,0:T(8,128)(2,1)} %bitcast.23, bf16[4096,128]{1,0:T(8,128)(2,1)} %bitcast.17, bf16[4096,128]{1,0:T(8,128)(2,1)} %bitcast.18, s32[8,128]{1,0:T(8,128)} %bitcast.27, ...), custom_call_target="tpu_custom_call" | custom-call | tf_op jit(solution)/shard_map/layer/pallas_call | solution.py:626
  93.6 0.0 copy-start
  93.6 1.5 %copy.23 = bf16[1,32,1024]{2,1,0:T(8,128)(2,1)} copy(bf16[1,32,1024]{2,1,0:T(8,128)(2,1)} %bitcast.25) | data formatting | bytes 131072
  95.1 0.0 copy-done
  95.1 0.6 copy.24
Async XLA Ops:
  93.6 1.5 %copy-start = (f32[96,128]{1,0:T(8,128)S(1)}, f32[96,128]{1,0:T(8,128)}, u32[]{:S(2)}) copy-start(f32[96,128]{1,0:T(8,128)} %get-tuple-element.5) | copy-start | bytes 147460
